TPU v7x, 128 devices: a whole 4x4x4 slice. The times are simulated.
128 devices in a mesh: tbl: 16 (over z, y), row: 8 (over x, core).
Axes of the slice: x: 4, y: 4, z: 4, core: 2. Of those that a mesh axis runs over, the one named last changes fastest.
Arguments:
- slab: bfloat16 [8192, 256], P(('tbl', 'row')), may hold values from -1.1953125 to 1.1953125
- counts: int32 [16384, 8192], P(None, ('tbl', 'row')), may hold values 0 or 1
- cross_down: bfloat16 [4096, 512], replicated, may hold values from -0.09375 to 0.09375
- cross_up: bfloat16 [512, 4096], replicated, may hold values from -0.25 to 0.25
- cross_bias: float32 [4096], replicated, may hold values from -3 to 3
- out_weight: float32 [4096], replicated, may hold values from -0.09375 to 0.09375
- labels: int32 [16384], P(('tbl', 'row')), may hold values 0 or 1
Outputs:
- grad_slab: float32 [8192, 256], P(('tbl', 'row'))
- grad_down: bfloat16 [4096, 512], P(('tbl', 'row'))
- grad_up: bfloat16 [512, 4096], P(None, ('tbl', 'row'))
- grad_bias: float32 [4096], P(('tbl', 'row'))
- grad_out: float32 [4096], P(('tbl', 'row'))
All inputs are finite; a program needn't handle non-finite values. No bound on the sum of `counts` or of `labels` on one device may be relied on, other than what follows from the above.
Results may differ from a plain program's by a relative error of at most 0.022.
Values may be sent and summed in bfloat16 or wider, within the bound.
No kernel may reach another device: no remote copies, remote signals or barrier semaphores. Data moves between devices by JAX's collectives and lax.ppermute only.
A program may use at most 128 MiB of HBM per device.

v0:
```python
import jax
import jax.numpy as jnp
from jax import lax
from jax.experimental import pallas as pl
from jax.experimental.pallas import tpu as pltpu
from jax.sharding import Mesh
from jax.sharding import PartitionSpec as P


ALL = ("z", "y", "x", "c")
PLANE = ("y", "x", "c")
NZ, NY, NX, NC = 4, 4, 4, 2
NK = NX * NC
PEERS = NY * NK
OWN = 128
ROWS = 64
EMBED = 256
RANK = 512
COLS = 1024
SAMPLES = NZ * OWN
EXT = 16
PACK = 400
HALF = EMBED // 2
LATE = SAMPLES // 2
ORDER = ((0, 2, 1, 3), (0, 2, 3, 1))
PLACES = ((0, 2, 1, 3), (0, 3, 1, 2))
F32 = jnp.float32
BF16 = jnp.bfloat16


def dot(a, b, da, db):
    return lax.dot_general(a, b, (((da,), (db,)), ((), ())), preferred_element_type=F32)


def flat(z, y, x, c):
    return (((z % NZ) * NY + y % NY) * NX + x % NX) * NC + c % NC


def shift(value, dz=(0, 0), dc=0):
    pairs = [
        (flat(z, y, x, c), flat(z + dz[c], y, x, c + dc))
        for z in range(NZ)
        for y in range(NY)
        for x in range(NX)
        for c in range(NC)
    ]
    return lax.ppermute(value, ALL, pairs)


def near(value):
    return pltpu.with_memory_space_constraint(value, pltpu.VMEM)


def far(value):
    return pltpu.with_memory_space_constraint(value, pltpu.HBM)


def call(body, outs, args, specs=None, scratch=(), mib=24, cost=None):
    return pl.pallas_call(
        body,
        in_specs=specs or [pl.BlockSpec(memory_space=pltpu.VMEM)] * len(args),
        out_specs=[pl.BlockSpec(memory_space=pltpu.VMEM)] * len(outs),
        out_shape=outs,
        scratch_shapes=list(scratch),
        compiler_params=pltpu.CompilerParams(vmem_limit_bytes=mib << 20),
        cost_estimate=cost,
    )(*args)


IN_SMEM = pl.BlockSpec(memory_space=pltpu.SMEM)
IN_VMEM = pl.BlockSpec(memory_space=pltpu.VMEM)
IN_HBM = pl.BlockSpec(memory_space=pltpu.HBM)


def pack_counts(place, counts_t, slab):
    strip = NK * OWN

    def body(place_ref, counts_ref, slab_ref, out, held, slab_s, sems, slab_sem):
        def copy(y, n):
            z = lax.rem(place_ref[0] + n, NZ)
            start = pl.multiple_of(z * (NY * strip) + y * strip, strip)
            return pltpu.make_async_copy(counts_ref.at[:, pl.ds(start, strip)], held.at[y, n], sems.at[y, n])

        slab_copy = pltpu.make_async_copy(slab_ref, slab_s, slab_sem)
        slab_copy.start()
        for y in range(NY):
            for n in range(NZ):
                copy(y, n).start()
        slab_copy.wait()
        for k in range(PEERS):
            half = k % NC
            out[k, :, SAMPLES:] = slab_s[:, half * HALF : (half + 1) * HALF]
        for y in range(NY):
            for n in range(NZ):
                copy(y, n).wait()
                for k in range(NK):
                    to = PLACES[k % NC][n] * OWN
                    out[y * NK + k, :, to : to + OWN] = (
                        held[y, n, :, k * OWN : (k + 1) * OWN].astype(F32).astype(BF16)
                    )

    return call(
        body,
        [pltpu.VMEM((PEERS, ROWS, SAMPLES + HALF), BF16)],
        (place, far(counts_t), far(slab)),
        [IN_SMEM, IN_HBM, IN_HBM],
        [
            pltpu.VMEM((NY, NZ, ROWS, strip), jnp.int32),
            pltpu.VMEM((ROWS, EMBED), BF16),
            pltpu.SemaphoreType.DMA((NY, NZ)),
            pltpu.SemaphoreType.DMA,
        ],
    )[0]


def prepare(place, down, up, w, bias):
    def body(place_ref, down_ref, up_ref, w_ref, bias_ref, rows_out):
        here = pl.ds(pl.multiple_of(place_ref[0] * COLS, COLS), COLS)
        w = w_ref[:, here]
        for part in range(4):
            at = slice(part * 128, (part + 1) * 128)
            rows_out[at, :] = down_ref[here, at].T
        rows_out[RANK : 2 * RANK, :] = (up_ref[:, here].astype(F32) * w).astype(BF16)
        v = w * (1.0 + bias_ref[:, here])
        high = v.astype(BF16).astype(F32)
        at = lax.broadcasted_iota(jnp.int32, (EXT, COLS), 0)
        rows_out[2 * RANK :, :] = jnp.where(at < 2, high, jnp.where(at == 2, v - high, 0.0)).astype(BF16)

    return call(
        body,
        [pltpu.VMEM((2 * RANK + EXT, COLS), BF16)],
        (place, *(near(v) for v in (down, up, w, bias))),
        [IN_SMEM] + [IN_VMEM] * 4,
        cost=pl.CostEstimate(flops=1 << 29, bytes_accessed=6 << 20, transcendentals=0),
    )[0]


def prepare_own(place, up, w, bias):
    def body(place_ref, up_ref, w_ref, bias_ref, own_out, up_out):
        k = place_ref[2] * NC + place_ref[3]
        start = place_ref[0] * COLS + (place_ref[1] * 2 + lax.div(k, 4)) * 128
        strip = pl.ds(pl.multiple_of(start, 128), 128)
        offset = lax.rem(k, 4) * 32
        lane = lax.broadcasted_iota(jnp.int32, (32, 128), 1)
        row = lax.broadcasted_iota(jnp.int32, (32, 128), 0)
        own = lane == row + offset
        w_own = jnp.sum(jnp.where(own, w_ref[:, strip], 0.0), axis=1, keepdims=True)
        bias_own = jnp.sum(jnp.where(own, bias_ref[:, strip], 0.0), axis=1, keepdims=True)
        place_own = (row + place_ref[2] * 32).astype(F32)
        own_out[...] = jnp.where(lane == 0, w_own, jnp.where(lane == 1, bias_own, place_own))
        up_out[...] = dot(jnp.where(own, 1.0, 0.0).astype(BF16), up_ref[:, strip], 1, 1)

    return call(
        body,
        [pltpu.VMEM((32, 128), F32), pltpu.VMEM((32, RANK), F32)],
        (place, *(near(v) for v in (up, w, bias))),
        [IN_SMEM] + [IN_VMEM] * 3,
        cost=pl.CostEstimate(flops=1 << 27, bytes_accessed=1 << 20, transcendentals=0),
    )


def pool_half(arrived):
    def body(in_ref, pooled_ref):
        for y in range(NY):
            at = slice(y * 512, (y + 1) * 512)
            half = slice(y * HALF, (y + 1) * HALF)
            pooled_ref[half, :] = dot(in_ref[at, SAMPLES:].T, in_ref[at, :SAMPLES], 1, 0).astype(BF16)

    return call(
        body,
        [pltpu.VMEM((NY * HALF, SAMPLES), BF16)],
        (near(arrived),),
        cost=pl.CostEstimate(flops=1 << 29, bytes_accessed=2 << 20, transcendentals=0),
    )[0]


def head_of(rows_ref, pooled):
    head = dot(rows_ref[2 * RANK :, :], pooled, 1, 0)
    sums = head[0:1] + head[2:3]
    high = sums.astype(BF16).astype(F32)
    at = lax.broadcasted_iota(jnp.int32, (EXT, pooled.shape[1]), 0)
    return jnp.where(at == 0, high, jnp.where(at == 1, sums - high, 0.0)).astype(BF16)


def products(rows_ref, pooled, outs):
    for part in range(4):
        at = slice(part * 256, (part + 1) * 256)
        product = dot(rows_ref[at, :], pooled, 1, 0).astype(BF16)
        for i, out in enumerate(outs):
            out[at, :] = product[:, i * OWN : (i + 1) * OWN]
    ext = head_of(rows_ref, pooled)
    for i, out in enumerate(outs):
        out[2 * RANK :, :] = ext[:, i * OWN : (i + 1) * OWN]


def forward_far(place, arrived, other, half, rows):
    def body(place_ref, in_ref, other_ref, half_ref, rows_ref, pooled_ref, out):
        core = place_ref[3]
        for y in range(NY):
            at = slice(y * 512, (y + 1) * 512)
            mine = pl.multiple_of(y * EMBED + core * HALF, HALF)
            partners = pl.multiple_of(y * EMBED + (1 - core) * HALF, HALF)
            pooled_ref[pl.ds(mine, HALF), :] = half_ref[y * HALF : (y + 1) * HALF, :]
            pooled_ref[pl.ds(partners, HALF), :] = dot(
                other_ref[at, :].T, in_ref[at, :SAMPLES], 1, 0
            ).astype(BF16)
        products(rows_ref, pooled_ref[:, OWN : 2 * OWN], (out,))

    return call(
        body,
        [pltpu.VMEM((COLS, SAMPLES), BF16), pltpu.VMEM((2 * RANK + EXT, OWN), BF16)],
        (place, near(arrived), near(other), near(half), near(rows)),
        [IN_SMEM] + [IN_VMEM] * 4,
        cost=pl.CostEstimate(flops=3 << 30, bytes_accessed=4 << 20, transcendentals=0),
    )


def forward_near(pooled, rows):
    def body(pooled_ref, rows_ref, *outs):
        products(rows_ref, pooled_ref[:, 2 * OWN :], outs)

    return call(
        body,
        [pltpu.VMEM((2 * RANK + EXT, OWN), BF16)] * 2,
        (near(pooled), near(rows)),
        cost=pl.CostEstimate(flops=1 << 30, bytes_accessed=2 << 20, transcendentals=0),
    )


def forward_own(pooled, rows):
    def body(pooled_ref, rows_ref, out):
        products(rows_ref, pooled_ref[:, :OWN], (out,))

    return call(
        body,
        [pltpu.VMEM((2 * RANK + EXT, OWN), BF16)],
        (near(pooled), near(rows)),
        cost=pl.CostEstimate(flops=1 << 30, bytes_accessed=1 << 20, transcendentals=0),
    )[0]


def own_samples(parts, labels):
    def body(p0, p1, p2, p3, labels_ref, out):
        def total(rows):
            a, b, c, d = (p[rows, :].astype(F32) for p in (p0, p1, p2, p3))
            return (a + b) + (c + d)

        squeezed = total(slice(0, RANK)).astype(BF16).astype(F32)
        other = total(slice(RANK, 2 * RANK))
        ext = total(slice(2 * RANK, 2 * RANK + EXT))
        logits = ext[0:1] + ext[1:2] + jnp.sum(squeezed * other, axis=0, keepdims=True)
        g = jax.nn.sigmoid(logits) - labels_ref[...].astype(F32)
        out[0:RANK, :] = (g * other).astype(BF16)
        out[RANK : 2 * RANK, :] = (g * squeezed).astype(BF16)
        high = g.astype(BF16).astype(F32)
        at = lax.broadcasted_iota(jnp.int32, (EXT, OWN), 0)
        rows = jnp.where((at == 0) | (at == 2), high, jnp.where(at == 1, g - high, 0.0))
        out[2 * RANK :, :] = rows.astype(BF16)

    return call(body, [pltpu.VMEM((2 * RANK + EXT, OWN), BF16)], (*(near(p) for p in parts), labels))[0]


def by_sample(*blocks):
    return jnp.concatenate([b[...].T for b in blocks], axis=0)


def grad_pooled_of(g, rows_ref):
    tables = [slice(y * EMBED, (y + 1) * EMBED) for y in range(NY)]
    return [dot(g, rows_ref[:, table], 1, 0).astype(BF16) for table in tables]


def by_core(low_core, value, width):
    pairs = value.reshape(-1, NC, width, value.shape[1])
    even, odd = (pairs[:, c].reshape(-1, value.shape[1]) for c in range(NC))
    return jnp.where(low_core, even, odd), jnp.where(low_core, odd, even)


def late_values(place, pooled, arrived):
    def body(place_ref, pooled_ref, in_ref, mine, theirs):
        low_core = place_ref[3] == 0
        half = COLS // NC
        mine[:half, :], theirs[:half, :] = by_core(low_core, pooled_ref[:, LATE:], 32)
        for y in range(NY):
            rows = slice(half + y * 256, half + (y + 1) * 256)
            counts = in_ref[y * 512 : (y + 1) * 512, LATE:SAMPLES]
            mine[rows, :], theirs[rows, :] = by_core(low_core, counts, ROWS)

    return call(
        body,
        [pltpu.VMEM((COLS // NC + NY * 256, SAMPLES - LATE), BF16)] * 2,
        (place, near(pooled), near(arrived)),
        [IN_SMEM] + [IN_VMEM] * 2,
        cost=pl.CostEstimate(flops=1 << 27, bytes_accessed=2 << 20, transcendentals=0),
    )


def put_weights(out, first, j, value):
    for h in range(2):
        at = first + (2 * j + h) * 32
        held = value[:, h * 128 : (h + 1) * 128].reshape(NY * NX, 32, 128)
        out(slice(0, NY * NX), slice(at, at + 32), held)


def put_sums(out, first, value):
    for y in range(NY):
        row = value[:, y * 128 : (y + 1) * 128]
        for x in range(NX):
            out(y * NX + x, slice(first, first + EXT), row)


def put_slab(out, y, value):
    for h in range(2):
        held = value[:, h * 128 : (h + 1) * 128].reshape(NX, ROWS, 128)
        out(slice(y * NX, (y + 1) * NX), slice(h * ROWS, (h + 1) * ROWS), held)


def backward_first(place, block0, block1, pooled, arrived, rows):
    def body(place_ref, b0, b1, pooled_ref, in_ref, rows_ref, mine, theirs):
        low_core = place_ref[3] == 0
        g = by_sample(b0, b1)
        products = grad_pooled_of(g, rows_ref)
        ext = jnp.concatenate([b0[2 * RANK :, :], b1[2 * RANK :, :]], axis=1)

        def writer(ref):
            def write(targets, at, value):
                ref[targets, at, :] = value.astype(ref.dtype)

            return write

        outs = [writer(mine), writer(theirs)]
        for out, part in zip(outs, by_core(low_core, pooled_ref[:, :LATE], 32)):
            for j in range(4):
                put_weights(out, 2 * ROWS, j, dot(part, g[:, j * 256 : (j + 1) * 256], 1, 0))
            put_sums(out, 384, dot(ext, part, 1, 1))
        for y, grad_pooled in enumerate(products):
            counts = in_ref[y * 512 : (y + 1) * 512, :LATE]
            for out, part in zip(outs, by_core(low_core, counts, ROWS)):
                put_slab(out, y, dot(part, grad_pooled, 1, 0))

    return call(
        body,
        [pltpu.VMEM((NY * NX, PACK, 128), F32), pltpu.VMEM((NY * NX, PACK, 128), BF16)],
        (place, *(near(v) for v in (block0, block1, pooled, arrived, rows))),
        [IN_SMEM] + [IN_VMEM] * 5,
        cost=pl.CostEstimate(flops=2 << 30, bytes_accessed=6 << 20, transcendentals=0),
    )


def late_products(block2, block3, rows):
    def body(b2, b3, rows_ref, g_out, out):
        g = by_sample(b2, b3)
        g_out[...] = g
        for y, grad_pooled in enumerate(grad_pooled_of(g, rows_ref)):
            out[:, y * EMBED : (y + 1) * EMBED] = grad_pooled

    return call(
        body,
        [pltpu.VMEM((SAMPLES - LATE, 2 * RANK + EXT), BF16), pltpu.VMEM((SAMPLES - LATE, COLS), BF16)],
        tuple(near(v) for v in (block2, block3, rows)),
        cost=pl.CostEstimate(flops=1 << 30, bytes_accessed=4 << 20, transcendentals=0),
    )


def late_own(g, blocks, values, first):
    def body(g_ref, b2, b3, own_ref, first_ref, out):
        pooled = own_ref[: COLS // NC, :]

        def write(targets, at, value):
            shifted = slice(at.start + 2 * ROWS, at.stop + 2 * ROWS)
            out[targets, at, :] = first_ref[targets, shifted, :] + value

        for j in range(4):
            put_weights(write, 0, j, dot(pooled, g_ref[:, j * 256 : (j + 1) * 256], 1, 0))
        ext = jnp.concatenate([b2[2 * RANK :, :], b3[2 * RANK :, :]], axis=1)
        put_sums(write, 256, dot(ext, pooled, 1, 1))

    return call(
        body,
        [pltpu.VMEM((NY * NX, PACK - 2 * ROWS, 128), F32)],
        tuple(near(v) for v in (g, *blocks, values, first)),
        cost=pl.CostEstimate(flops=1 << 30, bytes_accessed=4 << 20, transcendentals=0),
    )[0]


def late_weights(blocks, values, so_far, first):
    def body(b2, b3, values_ref, so_far_ref, first_ref, out):
        pooled = values_ref[: COLS // NC, :]
        g = by_sample(b2, b3)

        def write(targets, at, value):
            shifted = slice(at.start + 2 * ROWS, at.stop + 2 * ROWS)
            held = so_far_ref[targets, at, :] + first_ref[targets, shifted, :].astype(F32)
            out[targets, at, :] = (held + value).astype(BF16)

        for j in range(4):
            put_weights(write, 0, j, dot(pooled, g[:, j * 256 : (j + 1) * 256], 1, 0))
        ext = jnp.concatenate([b2[2 * RANK :, :], b3[2 * RANK :, :]], axis=1)
        put_sums(write, 256, dot(ext, pooled, 1, 1))

    return call(
        body,
        [pltpu.VMEM((NY * NX, PACK - 2 * ROWS, 128), BF16)],
        tuple(near(v) for v in (*blocks, values, so_far, first)),
        cost=pl.CostEstimate(flops=1 << 30, bytes_accessed=4 << 20, transcendentals=0),
    )[0]


def late_slab(products, partner_products, values, partner_values, first, partner_first, weights):
    def body(own_products, their_products, own_ref, partner_ref, first_ref, other_ref, weights_ref, out):
        half = COLS // NC
        out[:, 2 * ROWS :, :] = weights_ref[...]

        def write(targets, at, value):
            held = first_ref[targets, at, :] + other_ref[targets, at, :].astype(F32)
            out[targets, at, :] = (held + value).astype(BF16)

        for y in range(NY):
            rows = slice(half + y * 256, half + (y + 1) * 256)
            table = slice(y * EMBED, (y + 1) * EMBED)
            counts = jnp.concatenate([own_ref[rows, :], partner_ref[rows, :]], axis=1)
            both = jnp.concatenate([own_products[:, table], their_products[:, table]], axis=0)
            put_slab(write, y, dot(counts, both, 1, 0))

    return call(
        body,
        [pltpu.VMEM((NY * NX, PACK, 128), BF16)],
        tuple(
            near(v)
            for v in (products, partner_products, values, partner_values, first, partner_first, weights)
        ),
        cost=pl.CostEstimate(flops=1 << 29, bytes_accessed=4 << 20, transcendentals=0),
    )[0]


def finish(shares, own, up_own):
    def body(in_ref, own_ref, up_ref, slab_out, down_out, up_out, bias_out, out_out):
        def total(at):
            held = [(in_ref[i, at, :] + in_ref[i + 1, at, :]).astype(F32) for i in range(0, NY * NX, 2)]
            while len(held) > 1:
                held = [a + b for a, b in zip(held[::2], held[1::2])]
            return held[0]

        slab_out[:, :128] = total(slice(0, ROWS))
        slab_out[:, 128:] = total(slice(ROWS, 2 * ROWS))
        both = [total(slice(128 + j * 32, 160 + j * 32)) for j in range(8)]
        for j in range(4):
            down_out[:, j * 128 : (j + 1) * 128] = both[j].astype(BF16)
        product = jnp.concatenate(both[4:], axis=1)
        w_own, bias_own = own_ref[:, 0:1], own_ref[:, 1:2]
        up_out[...] = (product * w_own).astype(BF16)
        lane = lax.broadcasted_iota(jnp.int32, (32, 128), 1)
        row = lax.broadcasted_iota(jnp.int32, (32, 128), 0)
        last = total(slice(384, 400))
        own = lane.astype(F32) == own_ref[:, 2:3]
        sums = jnp.sum(jnp.where(own, last[0:1] + last[1:2], 0.0), axis=1, keepdims=True)
        out = (1.0 + bias_own) * sums + jnp.sum(product * up_ref[...], axis=1, keepdims=True)
        bias_out[...] = jnp.sum(jnp.where(lane == row, w_own * sums, 0.0), axis=0, keepdims=True)[:, :32]
        out_out[...] = jnp.sum(jnp.where(lane == row, out, 0.0), axis=0, keepdims=True)[:, :32]

    return call(
        body,
        [
            jax.ShapeDtypeStruct((ROWS, EMBED), F32),
            jax.ShapeDtypeStruct((32, RANK), BF16),
            jax.ShapeDtypeStruct((32, RANK), BF16),
            jax.ShapeDtypeStruct((1, 32), F32),
            jax.ShapeDtypeStruct((1, 32), F32),
        ],
        (near(shares), near(own), near(up_own)),
    )


def local(slab, counts, cross_down, cross_up, cross_bias, out_weight, labels):
    place = jnp.stack([lax.axis_index(a) for a in ALL]).astype(jnp.int32)
    w_row, bias_row = out_weight.reshape(1, -1), cross_bias.reshape(1, -1)
    rows = prepare(place, cross_down, cross_up, w_row, bias_row)
    own, up_own = prepare_own(place, cross_up, w_row, bias_row)
    sent = pack_counts(place, counts.T, slab)
    arrived = lax.all_to_all(sent, PLANE, 0, 0, tiled=True).reshape(PEERS * ROWS, SAMPLES + HALF)
    other = shift(arrived[:, SAMPLES:], dc=1)
    half = pool_half(arrived)
    pooled, chunk1 = forward_far(place, arrived, other, half, rows)
    part1 = shift(chunk1, dz=(ORDER[0][1], ORDER[1][1]))
    chunk2, chunk3 = forward_near(pooled, rows)
    part2 = shift(chunk2, dz=(ORDER[0][2], ORDER[1][2]))
    part3 = shift(chunk3, dz=(ORDER[0][3], ORDER[1][3]))
    parts = [part1, part2, part3]
    chunk = forward_own(pooled, rows)
    values, theirs = late_values(place, pooled, arrived)
    partner_values = shift(theirs, dc=1)
    block0 = own_samples([chunk] + parts, labels.reshape(1, OWN))
    blocks = []
    for i in range(1, NZ):
        blocks.append(shift(block0, dz=(-ORDER[0][i], -ORDER[1][i])))
    block1, *late = blocks
    first, theirs = backward_first(place, block0, block1, pooled, arrived, rows)
    partner_first = shift(theirs, dc=1)
    partner_late = []
    for block in late:
        partner_late.append(shift(block, dc=1))
    g, products = late_products(*late, rows)
    partner_products = shift(products, dc=1)
    so_far = late_own(g, late, values, first)
    weights = late_weights(partner_late, partner_values, so_far, partner_first)
    summed = late_slab(products, partner_products, values, partner_values, first, partner_first, weights)
    shares = lax.all_to_all(summed, ("y", "x"), 0, 0, tiled=True)
    grad_slab, grad_down, grad_up, grad_bias, grad_out = finish(shares, own, up_own)
    return grad_slab, grad_down, grad_up.T, grad_bias.reshape(32), grad_out.reshape(32)


def solution(mesh):
    torus = Mesh(mesh.devices.reshape(NZ, NY, NX, NC), ALL)
    return jax.shard_map(
        local,
        mesh=torus,
        in_specs=(P(ALL, None), P(None, ALL), P(), P(), P(), P(), P(ALL)),
        out_specs=(P(ALL, None), P(ALL, None), P(None, ALL), P(ALL), P(ALL)),
        check_vma=False,
    )
```

profile of v0, /device:TPU:0, one launch (start us, length us, event | category | flops | bytes accessed | tf_op | source)
XLA Modules:
  0.0 127.8 jit_solution(7594282890702477167)
XLA Ops:
  0.6 0.1 pad_add_fusion.place_ref
  0.7 0.0 copy-start.2
  0.7 3.3 %shard_map.110 = bf16[32,64,640]{2,1,0:T(8,128)(2,1)S(1)} custom-call(s32[4]{0:T(128)S(1)} %pad_add_fusion.place_ref, s32[64,16384]{1,0:T(8,128)} %bitcast.22, bf16[64,256]{1,0:T(8,128)(2,1)} %slab_ref.1), custom_call_target="tpu_custom_call" | custom-call | tf_op jit(solution)/shard_map/pallas_call | solution.py:59
  4.0 0.0 copy-start
  4.1 0.0 copy-start.3
  4.1 0.0 copy-start.4
  4.1 41.6 %all_to_all.10 = bf16[32,64,640]{2,1,0:T(8,128)(2,1)S(1)} all-to-all(bf16[32,64,640]{2,1,0:T(8,128)(2,1)S(1)} %shard_map.110), channel_id=1, replica_groups=mesh['z'=4,'y'=4,'x'=4,'c'=2] {'y','x','c'}, dimensions={0} | all-to-all | bytes 5242880 | tf_op jit(solution)/shard_map/all_to_all | solution.py:479
  45.7 0.2 collective-permute-start
  45.9 0.0 copy-done.2
  45.9 0.0 copy-done
  45.9 0.0 copy-done.3
  45.9 0.0 copy-done.4
  45.9 1.2 shard_map.112.rows_ref
  47.1 0.5 shard_map.111.half_ref
  47.5 0.1 collective-permute-done.other_ref
  47.7 1.8 %shard_map.113 = (bf16[1024,512]{1,0:T(8,128)(2,1)S(1)}, bf16[1040,128]{1,0:T(8,128)(2,1)S(1)}) custom-call(s32[4]{0:T(128)S(1)} %pad_add_fusion.place_ref, bf16[2048,640]{1,0:T(8,128)(2,1)S(1)} %bitcast.14, bf16[2048,128]{1,0:T(8,128)(2,1)S(1)} %collective-permute-done.other_ref, bf16[512,512]{1,0:T(8,128)(2,1)S(1)} %shard_map.111.half_ref, ...), custom_call_target="tpu_custom_call" | custom-call | flops 3221225472 | bytes 4194304 | tf_op jit(solution)/shard_map/pallas_call | solution.py:59
  49.4 0.8 shard_map.115
  50.2 0.0 copy-start.5
  50.3 2.0 %collective-permute-start.2 = (bf16[1040,128]{1,0:T(8,128)(2,1)S(1)}, bf16[1040,128]{1,0:T(8,128)(2,1)S(1)}, u32[]{:S(2)}, u32[]{:S(2)}) collective-permute-start(bf16[1040,128]{1,0:T(8,128)(2,1)S(1)} %get-tuple-element.24), channel_id=1, source_target_pairs={{0,32},{1,97},{2,34},{3,99},{4,36},{5,101},{6,38},{7,103},{8,40},{... | collective-permute-start | bytes 798728 | tf_op jit(solution)/shard_map/ppermute | solution.py:47
  52.2 2.2 %collective-permute-start.3 = (bf16[1040,128]{1,0:T(8,128)(2,1)S(1)}, bf16[1040,128]{1,0:T(8,128)(2,1)S(1)}, u32[]{:S(2)}, u32[]{:S(2)}) collective-permute-start(bf16[1040,128]{1,0:T(8,128)(2,1)S(1)} %get-tuple-element.25), channel_id=1, source_target_pairs={{0,96},{1,33},{2,98},{3,35},{4,100},{5,37},{6,102},{7,39},{8,104},... | collective-permute-start | bytes 798728 | tf_op jit(solution)/shard_map/ppermute | solution.py:47
  54.4 1.8 %collective-permute-start.1 = (bf16[1040,128]{1,0:T(8,128)(2,1)S(1)}, bf16[1040,128]{1,0:T(8,128)(2,1)S(1)}, u32[]{:S(2)}, u32[]{:S(2)}) collective-permute-start(bf16[1040,128]{1,0:T(8,128)(2,1)S(1)} %get-tuple-element.23), channel_id=1, source_target_pairs={{0,64},{1,65},{2,66},{3,67},{4,68},{5,69},{6,70},{7,71},{8,72},{9,... | collective-permute-start | bytes 798728 | tf_op jit(solution)/shard_map/ppermute | solution.py:47
  56.2 0.7 shard_map.114.p0
  57.0 2.4 %collective-permute-done.2.p2 = bf16[1040,128]{1,0:T(8,128)(2,1)S(1)} collective-permute-done((bf16[1040,128]{1,0:T(8,128)(2,1)S(1)}, bf16[1040,128]{1,0:T(8,128)(2,1)S(1)}, u32[]{:S(2)}, u32[]{:S(2)}) %collective-permute-start.2) | collective-permute-done | bytes 266272 | tf_op jit(solution)/shard_map/ppermute | solution.py:47
  59.4 6.8 %collective-permute-done.3.p3 = bf16[1040,128]{1,0:T(8,128)(2,1)S(1)} collective-permute-done((bf16[1040,128]{1,0:T(8,128)(2,1)S(1)}, bf16[1040,128]{1,0:T(8,128)(2,1)S(1)}, u32[]{:S(2)}, u32[]{:S(2)}) %collective-permute-start.3) | collective-permute-done | bytes 266272 | tf_op jit(solution)/shard_map/ppermute | solution.py:47
  66.2 2.0 %collective-permute-done.1.p1 = bf16[1040,128]{1,0:T(8,128)(2,1)S(1)} collective-permute-done((bf16[1040,128]{1,0:T(8,128)(2,1)S(1)}, bf16[1040,128]{1,0:T(8,128)(2,1)S(1)}, u32[]{:S(2)}, u32[]{:S(2)}) %collective-permute-start.1) | collective-permute-done | bytes 266272 | tf_op jit(solution)/shard_map/ppermute | solution.py:47
  68.2 0.0 copy-done.5
  68.2 0.3 shard_map.116.b0
  68.5 0.1 collective-permute-start.8
  68.6 9.3 %collective-permute-done.8.b1 = bf16[1040,128]{1,0:T(8,128)(2,1)S(1)} collective-permute-done((bf16[1040,128]{1,0:T(8,128)(2,1)S(1)}, bf16[1040,128]{1,0:T(8,128)(2,1)S(1)}, u32[]{:S(2)}, u32[]{:S(2)}) %collective-permute-start.8) | collective-permute-done | bytes 266272 | tf_op jit(solution)/shard_map/ppermute | solution.py:47
  77.9 2.4 %shard_map.119 = (f32[16,400,128]{2,1,0:T(8,128)S(1)}, bf16[16,400,128]{2,1,0:T(8,128)(2,1)S(1)}) custom-call(s32[4]{0:T(128)S(1)} %pad_add_fusion.place_ref, bf16[1040,128]{1,0:T(8,128)(2,1)S(1)} %shard_map.116.b0, bf16[1040,128]{1,0:T(8,128)(2,1)S(1)} %collective-permute-done.8.b1, bf16[1024,512]{1,0:T(8,128)(2,1)S(1)} %get-tuple-element.22.pooled_ref, ...), custom_call_target="tpu_custom_call" | custom-call | flops 2147483648 | bytes 6291456 | tf_op jit(solution)/shard_map/pallas_call | solution.py:59
  80.3 0.1 collective-permute-start.9
  80.4 1.5 %collective-permute-start.4 = (bf16[1040,128]{1,0:T(8,128)(2,1)S(1)}, bf16[1040,128]{1,0:T(8,128)(2,1)S(1)}, u32[]{:S(2)}, u32[]{:S(2)}) collective-permute-start(bf16[1040,128]{1,0:T(8,128)(2,1)S(1)} %shard_map.116.b0), channel_id=1, source_target_pairs={{0,96},{1,33},{2,98},{3,35},{4,100},{5,37},{6,102},{7,39},{8,104},... | collective-permute-start | bytes 798728 | tf_op jit(solution)/shard_map/ppermute | solution.py:47
  81.9 0.6 collective-permute-start.5
  82.5 0.6 shard_map.118
  83.1 1.2 collective-permute-start.7
  84.3 4.9 %collective-permute-done.4.b2 = bf16[1040,128]{1,0:T(8,128)(2,1)S(1)} collective-permute-done((bf16[1040,128]{1,0:T(8,128)(2,1)S(1)}, bf16[1040,128]{1,0:T(8,128)(2,1)S(1)}, u32[]{:S(2)}, u32[]{:S(2)}) %collective-permute-start.4) | collective-permute-done | bytes 266272 | tf_op jit(solution)/shard_map/ppermute | solution.py:47
  89.2 1.2 collective-permute-done.5.b3
  90.4 0.9 shard_map.117
  91.3 0.1 collective-permute-start.6
  91.4 0.5 collective-permute-start.10
  91.9 0.1 collective-permute-start.11
  92.0 0.5 shard_map.120.so_far_ref
  92.4 0.0 collective-permute-done.7.values_ref.partner_ref
  92.4 1.2 collective-permute-done.10.b2
  93.6 0.4 collective-permute-done.11.b3
  94.0 0.0 collective-permute-done.9.first_ref.other_ref
  94.0 0.6 shard_map.121.weights_ref
  94.6 0.0 collective-permute-done.6.their_products
  94.6 1.7 %shard_map.122 = bf16[16,400,128]{2,1,0:T(8,128)(2,1)} custom-call(bf16[256,1024]{1,0:T(8,128)(2,1)S(1)} %get-tuple-element.26.own_products, bf16[256,1024]{1,0:T(8,128)(2,1)S(1)} %collective-permute-done.6.their_products, bf16[1536,256]{1,0:T(8,128)(2,1)S(1)} %get-tuple-element.27.own_ref, ...), custom_call_target="tpu_custom_call" | custom-call | flops 536870912 | bytes 4194304 | tf_op jit(solution)/shard_map/pallas_call | solution.py:59
  96.4 3.7 %all-to-all-start.1 = ((bf16[16,400,128]{2,1,0:T(8,128)(2,1)}), bf16[16,400,128]{2,1,0:T(8,128)(2,1)S(1)}, u32[]{:S(2)}, u32[]{:S(2)}) async-start(bf16[16,400,128]{2,1,0:T(8,128)(2,1)} %shard_map.122), calls=%async_computation.1 | async-start | bytes 3276800 | tf_op jit(solution)/shard_map/all_to_all | solution.py:506
  100.1 0.0 copy-start.1
  100.1 2.2 %copy-done.1 = bf16[512,4096]{1,0:T(8,128)(2,1)S(1)} copy-done((bf16[512,4096]{1,0:T(8,128)(2,1)S(1)}, bf16[512,4096]{1,0:T(8,128)(2,1)}, u32[]{:S(2)}) %copy-start.1) | copy-done | bytes 4194328
  102.3 0.7 shard_map.123
  103.0 23.9 %all-to-all-done.1.in_ref = bf16[16,400,128]{2,1,0:T(8,128)(2,1)S(1)} async-done(((bf16[16,400,128]{2,1,0:T(8,128)(2,1)}), bf16[16,400,128]{2,1,0:T(8,128)(2,1)S(1)}, u32[]{:S(2)}, u32[]{:S(2)}) %all-to-all-start.1) | async-done | bytes 1638432 | tf_op jit(solution)/shard_map/all_to_all | solution.py:506
  126.9 0.9 shard_map.124
  (1 shorter events, 0.0 us)
Async XLA Ops:
  0.7 45.2 %copy-start.2 = (bf16[4096,512]{1,0:T(8,128)(2,1)S(1)}, bf16[4096,512]{1,0:T(8,128)(2,1)}, u32[]{:S(2)}) copy-start(bf16[4096,512]{1,0:T(8,128)(2,1)} %down_ref.1) | copy-start | bytes 12582916
  4.0 41.8 %copy-start = (bf16[512,4096]{1,0:T(8,128)(2,1)S(1)}, bf16[512,4096]{1,0:T(8,128)(2,1)}, u32[]{:S(2)}) copy-start(bf16[512,4096]{1,0:T(8,128)(2,1)} %up_ref.3) | copy-start | bytes 12582916
  4.1 41.8 %copy-start.3 = (f32[4096]{0:T(1024)S(1)}, f32[4096]{0:T(1024)}, u32[]{:S(2)}) copy-start(f32[4096]{0:T(1024)} %param.12) | copy-start | bytes 49156
  4.1 41.8 %copy-start.4 = (f32[4096]{0:T(1024)S(1)}, f32[4096]{0:T(1024)}, u32[]{:S(2)}) copy-start(f32[4096]{0:T(1024)} %param.11) | copy-start | bytes 49156
  45.7 2.0 %collective-permute-start = (bf16[2048,128]{1,0:T(8,128)(2,1)S(1)}, bf16[2048,128]{1,0:T(8,128)(2,1)S(1)}, u32[]{:S(2)}, u32[]{:S(2)}) collective-permute-start(bf16[2048,128]{1,0:T(8,128)(2,1)S(1)} %slice.4), channel_id=1, source_target_pairs={{0,1},{1,0},{2,3},{3,2},{4,5},{5,4},{6,7},{7,6},{8,9},{9,8},{10,11... | collective-permute-start | bytes 1572872 | tf_op jit(solution)/shard_map/ppermute | solution.py:47
  50.2 18.0 %copy-start.5 = (s32[128]{0:T(128)S(1)}, s32[128]{0:T(128)}, u32[]{:S(2)}) copy-start(s32[128]{0:T(128)} %param.13) | copy-start | bytes 1540
  50.3 9.1 %collective-permute-start.2 = (bf16[1040,128]{1,0:T(8,128)(2,1)S(1)}, bf16[1040,128]{1,0:T(8,128)(2,1)S(1)}, u32[]{:S(2)}, u32[]{:S(2)}) collective-permute-start(bf16[1040,128]{1,0:T(8,128)(2,1)S(1)} %get-tuple-element.24), channel_id=1, source_target_pairs={{0,32},{1,97},{2,34},{3,99},{4,36},{5,101},{6,38},{7,103},{8,40},{... | collective-permute-start | bytes 798728 | tf_op jit(solution)/shard_map/ppermute | solution.py:47
  52.2 13.9 %collective-permute-start.3 = (bf16[1040,128]{1,0:T(8,128)(2,1)S(1)}, bf16[1040,128]{1,0:T(8,128)(2,1)S(1)}, u32[]{:S(2)}, u32[]{:S(2)}) collective-permute-start(bf16[1040,128]{1,0:T(8,128)(2,1)S(1)} %get-tuple-element.25), channel_id=1, source_target_pairs={{0,96},{1,33},{2,98},{3,35},{4,100},{5,37},{6,102},{7,39},{8,104},... | collective-permute-start | bytes 798728 | tf_op jit(solution)/shard_map/ppermute | solution.py:47
  54.4 13.8 %collective-permute-start.1 = (bf16[1040,128]{1,0:T(8,128)(2,1)S(1)}, bf16[1040,128]{1,0:T(8,128)(2,1)S(1)}, u32[]{:S(2)}, u32[]{:S(2)}) collective-permute-start(bf16[1040,128]{1,0:T(8,128)(2,1)S(1)} %get-tuple-element.23), channel_id=1, source_target_pairs={{0,64},{1,65},{2,66},{3,67},{4,68},{5,69},{6,70},{7,71},{8,72},{9,... | collective-permute-start | bytes 798728 | tf_op jit(solution)/shard_map/ppermute | solution.py:47
  68.5 9.4 %collective-permute-start.8 = (bf16[1040,128]{1,0:T(8,128)(2,1)S(1)}, bf16[1040,128]{1,0:T(8,128)(2,1)S(1)}, u32[]{:S(2)}, u32[]{:S(2)}) collective-permute-start(bf16[1040,128]{1,0:T(8,128)(2,1)S(1)} %shard_map.116.b0), channel_id=1, source_target_pairs={{0,64},{1,65},{2,66},{3,67},{4,68},{5,69},{6,70},{7,71},{8,72},{9,... | collective-permute-start | bytes 798728 | tf_op jit(solution)/shard_map/ppermute | solution.py:47
  80.3 13.7 %collective-permute-start.9 = (bf16[16,400,128]{2,1,0:T(8,128)(2,1)S(1)}, bf16[16,400,128]{2,1,0:T(8,128)(2,1)S(1)}, u32[]{:S(2)}, u32[]{:S(2)}) collective-permute-start(bf16[16,400,128]{2,1,0:T(8,128)(2,1)S(1)} %get-tuple-element.30), channel_id=1, source_target_pairs={{0,1},{1,0},{2,3},{3,2},{4,5},{5,4},{6,7},{7,6},{8,9},{9,8},{10,11... | collective-permute-start | bytes 4915208 | tf_op jit(solution)/shard_map/ppermute | solution.py:47
  80.4 8.8 %collective-permute-start.4 = (bf16[1040,128]{1,0:T(8,128)(2,1)S(1)}, bf16[1040,128]{1,0:T(8,128)(2,1)S(1)}, u32[]{:S(2)}, u32[]{:S(2)}) collective-permute-start(bf16[1040,128]{1,0:T(8,128)(2,1)S(1)} %shard_map.116.b0), channel_id=1, source_target_pairs={{0,96},{1,33},{2,98},{3,35},{4,100},{5,37},{6,102},{7,39},{8,104},... | collective-permute-start | bytes 798728 | tf_op jit(solution)/shard_map/ppermute | solution.py:47
  81.9 8.5 %collective-permute-start.5 = (bf16[1040,128]{1,0:T(8,128)(2,1)S(1)}, bf16[1040,128]{1,0:T(8,128)(2,1)S(1)}, u32[]{:S(2)}, u32[]{:S(2)}) collective-permute-start(bf16[1040,128]{1,0:T(8,128)(2,1)S(1)} %shard_map.116.b0), channel_id=1, source_target_pairs={{0,32},{1,97},{2,34},{3,99},{4,36},{5,101},{6,38},{7,103},{8,40},{... | collective-permute-start | bytes 798728 | tf_op jit(solution)/shard_map/ppermute | solution.py:47
  83.1 9.3 %collective-permute-start.7 = (bf16[1536,256]{1,0:T(8,128)(2,1)S(1)}, bf16[1536,256]{1,0:T(8,128)(2,1)S(1)}, u32[]{:S(2)}, u32[]{:S(2)}) collective-permute-start(bf16[1536,256]{1,0:T(8,128)(2,1)S(1)} %get-tuple-element.28), channel_id=1, source_target_pairs={{0,1},{1,0},{2,3},{3,2},{4,5},{5,4},{6,7},{7,6},{8,9},{9,8},{10,11... | collective-permute-start | bytes 2359304 | tf_op jit(solution)/shard_map/ppermute | solution.py:47
  91.3 3.3 %collective-permute-start.6 = (bf16[256,1024]{1,0:T(8,128)(2,1)S(1)}, bf16[256,1024]{1,0:T(8,128)(2,1)S(1)}, u32[]{:S(2)}, u32[]{:S(2)}) collective-permute-start(bf16[256,1024]{1,0:T(8,128)(2,1)S(1)} %get-tuple-element.26.own_products), channel_id=1, source_target_pairs={{0,1},{1,0},{2,3},{3,2},{4,5},{5,4},{6,7},{7,6},{8,9},{9,8},{10,11... | collective-permute-start | bytes 1572872 | tf_op jit(solution)/shard_map/ppermute | solution.py:47
  91.4 2.3 %collective-permute-start.10 = (bf16[1040,128]{1,0:T(8,128)(2,1)S(1)}, bf16[1040,128]{1,0:T(8,128)(2,1)S(1)}, u32[]{:S(2)}, u32[]{:S(2)}) collective-permute-start(bf16[1040,128]{1,0:T(8,128)(2,1)S(1)} %collective-permute-done.4.b2), channel_id=1, source_target_pairs={{0,1},{1,0},{2,3},{3,2},{4,5},{5,4},{6,7},{7,6},{8,9},{9,8},{10,11... | collective-permute-start | bytes 798728 | tf_op jit(solution)/shard_map/ppermute | solution.py:47
  91.9 2.2 %collective-permute-start.11 = (bf16[1040,128]{1,0:T(8,128)(2,1)S(1)}, bf16[1040,128]{1,0:T(8,128)(2,1)S(1)}, u32[]{:S(2)}, u32[]{:S(2)}) collective-permute-start(bf16[1040,128]{1,0:T(8,128)(2,1)S(1)} %collective-permute-done.5.b3), channel_id=1, source_target_pairs={{0,1},{1,0},{2,3},{3,2},{4,5},{5,4},{6,7},{7,6},{8,9},{9,8},{10,11... | collective-permute-start | bytes 798728 | tf_op jit(solution)/shard_map/ppermute | solution.py:47
  96.4 30.5 %all-to-all-start.1 = ((bf16[16,400,128]{2,1,0:T(8,128)(2,1)}), bf16[16,400,128]{2,1,0:T(8,128)(2,1)S(1)}, u32[]{:S(2)}, u32[]{:S(2)}) async-start(bf16[16,400,128]{2,1,0:T(8,128)(2,1)} %shard_map.122), calls=%async_computation.1 | async-start | bytes 3276800 | tf_op jit(solution)/shard_map/all_to_all | solution.py:506
  100.1 2.2 %copy-start.1 = (bf16[512,4096]{1,0:T(8,128)(2,1)S(1)}, bf16[512,4096]{1,0:T(8,128)(2,1)}, u32[]{:S(2)}) copy-start(bf16[512,4096]{1,0:T(8,128)(2,1)} %up_ref.3) | copy-start | bytes 12582916
where the time goes:
time: 128 us
  waiting for transfers between devices  52.3 us (41%)
  blocking collectives  41.6 us (32%)
  Pallas kernels  16.8 us (13%)
  starting transfers between devices  14 us (11%)
  local copies, waits for them, and re-layouts  2.25 us (2%)
    all_to_all x1, blocking collectives, local(): lax.all_to_all(sent, PLANE, 0, 0, tiled=True)  41.6 us
    ppermute x12, waiting for transfers between devices, shift(): return lax.ppermute(value, ALL, pairs)  28.4 us
    all_to_all x1, waiting for transfers between devices, local(): shares = lax.all_to_all(summed, ('y', 'x'), 0, 0, tiled=True)  23.9 us
    pallas_call x15, Pallas kernels, call(): pl.pallas_call(body, in_specs=specs or [pl.BlockSpec(memory_space=pltpu.V...  16.8 us
    ppermute x12, starting transfers between devices, shift(): return lax.ppermute(value, ALL, pairs)  10.3 us
    all_to_all x1, starting transfers between devices, local(): shares = lax.all_to_all(summed, ('y', 'x'), 0, 0, tiled=True)  3.71 us
  transfers between devices with their start and end apart: 13, of which 10 were waited for; matrix products, arithmetic and copies ran while one was open for 0% of the time, Pallas kernels for 4%

commit v1 on v0

--- a/solution.py
+++ b/solution.py
@@ -85,7 +85,7 @@
         slab_copy.start()
         for y in range(NY):
             for n in range(NZ):
-                copy(y, n).start()
+                copy(y, n).start(priority=n % 2)
         slab_copy.wait()
         for k in range(PEERS):
             half = k % NC
@@ -361,46 +361,26 @@
     )
 
 
-def late_own(g, blocks, values, first):
-    def body(g_ref, b2, b3, own_ref, first_ref, out):
-        pooled = own_ref[: COLS // NC, :]
+def late_weights(g, blocks, partner_blocks, values, partner_values, first, partner_first):
+    def body(g_ref, b2, b3, p2, p3, own_ref, partner_ref, first_ref, other_ref, out):
+        half = COLS // NC
+        pooled = jnp.concatenate([own_ref[:half, :], partner_ref[:half, :]], axis=1)
+        both = jnp.concatenate([g_ref[...], by_sample(p2, p3)], axis=0)
 
         def write(targets, at, value):
             shifted = slice(at.start + 2 * ROWS, at.stop + 2 * ROWS)
-            out[targets, at, :] = first_ref[targets, shifted, :] + value
+            held = first_ref[targets, shifted, :] + other_ref[targets, shifted, :].astype(F32)
+            out[targets, at, :] = (held + value).astype(BF16)
 
         for j in range(4):
-            put_weights(write, 0, j, dot(pooled, g_ref[:, j * 256 : (j + 1) * 256], 1, 0))
-        ext = jnp.concatenate([b2[2 * RANK :, :], b3[2 * RANK :, :]], axis=1)
+            put_weights(write, 0, j, dot(pooled, both[:, j * 256 : (j + 1) * 256], 1, 0))
+        ext = jnp.concatenate([b[2 * RANK :, :] for b in (b2, b3, p2, p3)], axis=1)
         put_sums(write, 256, dot(ext, pooled, 1, 1))
 
     return call(
         body,
-        [pltpu.VMEM((NY * NX, PACK - 2 * ROWS, 128), F32)],
-        tuple(near(v) for v in (g, *blocks, values, first)),
-        cost=pl.CostEstimate(flops=1 << 30, bytes_accessed=4 << 20, transcendentals=0),
-    )[0]
-
-
-def late_weights(blocks, values, so_far, first):
-    def body(b2, b3, values_ref, so_far_ref, first_ref, out):
-        pooled = values_ref[: COLS // NC, :]
-        g = by_sample(b2, b3)
-
-        def write(targets, at, value):
-            shifted = slice(at.start + 2 * ROWS, at.stop + 2 * ROWS)
-            held = so_far_ref[targets, at, :] + first_ref[targets, shifted, :].astype(F32)
-            out[targets, at, :] = (held + value).astype(BF16)
-
-        for j in range(4):
-            put_weights(write, 0, j, dot(pooled, g[:, j * 256 : (j + 1) * 256], 1, 0))
-        ext = jnp.concatenate([b2[2 * RANK :, :], b3[2 * RANK :, :]], axis=1)
-        put_sums(write, 256, dot(ext, pooled, 1, 1))
-
-    return call(
-        body,
         [pltpu.VMEM((NY * NX, PACK - 2 * ROWS, 128), BF16)],
-        tuple(near(v) for v in (*blocks, values, so_far, first)),
+        tuple(near(v) for v in (g, *blocks, *partner_blocks, values, partner_values, first, partner_first)),
         cost=pl.CostEstimate(flops=1 << 30, bytes_accessed=4 << 20, transcendentals=0),
     )[0]
 
@@ -435,10 +415,10 @@
 def finish(shares, own, up_own):
     def body(in_ref, own_ref, up_ref, slab_out, down_out, up_out, bias_out, out_out):
         def total(at):
-            held = [(in_ref[i, at, :] + in_ref[i + 1, at, :]).astype(F32) for i in range(0, NY * NX, 2)]
-            while len(held) > 1:
-                held = [a + b for a, b in zip(held[::2], held[1::2])]
-            return held[0]
+            held = in_ref[0, at, :].astype(F32)
+            for i in range(1, NY * NX):
+                held = held + in_ref[i, at, :].astype(F32)
+            return held
 
         slab_out[:, :128] = total(slice(0, ROWS))
         slab_out[:, 128:] = total(slice(ROWS, 2 * ROWS))
@@ -500,8 +480,7 @@
         partner_late.append(shift(block, dc=1))
     g, products = late_products(*late, rows)
     partner_products = shift(products, dc=1)
-    so_far = late_own(g, late, values, first)
-    weights = late_weights(partner_late, partner_values, so_far, partner_first)
+    weights = late_weights(g, late, partner_late, values, partner_values, first, partner_first)
     summed = late_slab(products, partner_products, values, partner_values, first, partner_first, weights)
     shares = lax.all_to_all(summed, ("y", "x"), 0, 0, tiled=True)
     grad_slab, grad_down, grad_up, grad_bias, grad_out = finish(shares, own, up_own)

time: 128 us -> 128 us (level)
    pallas_call x15 -> x14, Pallas kernels: 16.8 us -> 16.5 us  [call(): pl.pallas_call(body, in_specs=specs or [pl.BlockSpec(memory_space=pltpu.V...]
where the time goes in v1:
time: 128 us
  waiting for transfers between devices  52.8 us (41%)
  blocking collectives  41.6 us (32%)
  Pallas kernels  16.5 us (13%)
  starting transfers between devices  14 us (11%)
  local copies, waits for them, and re-layouts  2.25 us (2%)
    all_to_all x1, blocking collectives, local(): lax.all_to_all(sent, PLANE, 0, 0, tiled=True)  41.6 us
    ppermute x12, waiting for transfers between devices, shift(): return lax.ppermute(value, ALL, pairs)  28.9 us
    all_to_all x1, waiting for transfers between devices, local(): shares = lax.all_to_all(summed, ('y', 'x'), 0, 0, tiled=True)  23.9 us
    pallas_call x14, Pallas kernels, call(): pl.pallas_call(body, in_specs=specs or [pl.BlockSpec(memory_space=pltpu.V...  16.5 us
    ppermute x12, starting transfers between devices, shift(): return lax.ppermute(value, ALL, pairs)  10.3 us
    all_to_all x1, starting transfers between devices, local(): shares = lax.all_to_all(summed, ('y', 'x'), 0, 0, tiled=True)  3.71 us
  transfers between devices with their start and end apart: 13, of which 10 were waited for; matrix products, arithmetic and copies ran while one was open for 0% of the time, Pallas kernels for 4%

profile of v1, /device:TPU:0, one launch (start us, length us, event | category | flops | bytes accessed | tf_op | source)
XLA Modules:
  0.0 127.9 jit_solution(7996023364219066569)
XLA Ops:
  0.6 0.1 pad_add_fusion.place_ref
  0.7 0.0 copy-start.2
  0.7 3.1 %shard_map.110 = bf16[32,64,640]{2,1,0:T(8,128)(2,1)S(1)} custom-call(s32[4]{0:T(128)S(1)} %pad_add_fusion.place_ref, s32[64,16384]{1,0:T(8,128)} %bitcast.22, bf16[64,256]{1,0:T(8,128)(2,1)} %slab_ref.1), custom_call_target="tpu_custom_call" | custom-call | tf_op jit(solution)/shard_map/pallas_call | solution.py:59
  3.9 0.0 copy-start
  3.9 0.0 copy-start.3
  3.9 0.0 copy-start.4
  3.9 41.6 %all_to_all.10 = bf16[32,64,640]{2,1,0:T(8,128)(2,1)S(1)} all-to-all(bf16[32,64,640]{2,1,0:T(8,128)(2,1)S(1)} %shard_map.110), channel_id=1, replica_groups=mesh['z'=4,'y'=4,'x'=4,'c'=2] {'y','x','c'}, dimensions={0} | all-to-all | bytes 5242880 | tf_op jit(solution)/shard_map/all_to_all | solution.py:459
  45.5 0.2 collective-permute-start
  45.7 0.0 copy-done.2
  45.7 0.0 copy-done
  45.7 0.0 copy-done.3
  45.7 0.0 copy-done.4
  45.7 1.2 shard_map.112.rows_ref
  46.9 0.5 shard_map.111.half_ref
  47.3 0.1 collective-permute-done.other_ref
  47.5 1.8 %shard_map.113 = (bf16[1024,512]{1,0:T(8,128)(2,1)S(1)}, bf16[1040,128]{1,0:T(8,128)(2,1)S(1)}) custom-call(s32[4]{0:T(128)S(1)} %pad_add_fusion.place_ref, bf16[2048,640]{1,0:T(8,128)(2,1)S(1)} %bitcast.14, bf16[2048,128]{1,0:T(8,128)(2,1)S(1)} %collective-permute-done.other_ref, bf16[512,512]{1,0:T(8,128)(2,1)S(1)} %shard_map.111.half_ref, ...), custom_call_target="tpu_custom_call" | custom-call | flops 3221225472 | bytes 4194304 | tf_op jit(solution)/shard_map/pallas_call | solution.py:59
  49.2 0.8 shard_map.115
  50.1 0.0 copy-start.5
  50.1 2.0 %collective-permute-start.2 = (bf16[1040,128]{1,0:T(8,128)(2,1)S(1)}, bf16[1040,128]{1,0:T(8,128)(2,1)S(1)}, u32[]{:S(2)}, u32[]{:S(2)}) collective-permute-start(bf16[1040,128]{1,0:T(8,128)(2,1)S(1)} %get-tuple-element.24), channel_id=1, source_target_pairs={{0,32},{1,97},{2,34},{3,99},{4,36},{5,101},{6,38},{7,103},{8,40},{... | collective-permute-start | bytes 798728 | tf_op jit(solution)/shard_map/ppermute | solution.py:47
  52.1 2.2 %collective-permute-start.3 = (bf16[1040,128]{1,0:T(8,128)(2,1)S(1)}, bf16[1040,128]{1,0:T(8,128)(2,1)S(1)}, u32[]{:S(2)}, u32[]{:S(2)}) collective-permute-start(bf16[1040,128]{1,0:T(8,128)(2,1)S(1)} %get-tuple-element.25), channel_id=1, source_target_pairs={{0,96},{1,33},{2,98},{3,35},{4,100},{5,37},{6,102},{7,39},{8,104},... | collective-permute-start | bytes 798728 | tf_op jit(solution)/shard_map/ppermute | solution.py:47
  54.3 1.8 %collective-permute-start.1 = (bf16[1040,128]{1,0:T(8,128)(2,1)S(1)}, bf16[1040,128]{1,0:T(8,128)(2,1)S(1)}, u32[]{:S(2)}, u32[]{:S(2)}) collective-permute-start(bf16[1040,128]{1,0:T(8,128)(2,1)S(1)} %get-tuple-element.23), channel_id=1, source_target_pairs={{0,64},{1,65},{2,66},{3,67},{4,68},{5,69},{6,70},{7,71},{8,72},{9,... | collective-permute-start | bytes 798728 | tf_op jit(solution)/shard_map/ppermute | solution.py:47
  56.0 0.7 shard_map.114.p0
  56.8 2.4 %collective-permute-done.2.p2 = bf16[1040,128]{1,0:T(8,128)(2,1)S(1)} collective-permute-done((bf16[1040,128]{1,0:T(8,128)(2,1)S(1)}, bf16[1040,128]{1,0:T(8,128)(2,1)S(1)}, u32[]{:S(2)}, u32[]{:S(2)}) %collective-permute-start.2) | collective-permute-done | bytes 266272 | tf_op jit(solution)/shard_map/ppermute | solution.py:47
  59.2 6.8 %collective-permute-done.3.p3 = bf16[1040,128]{1,0:T(8,128)(2,1)S(1)} collective-permute-done((bf16[1040,128]{1,0:T(8,128)(2,1)S(1)}, bf16[1040,128]{1,0:T(8,128)(2,1)S(1)}, u32[]{:S(2)}, u32[]{:S(2)}) %collective-permute-start.3) | collective-permute-done | bytes 266272 | tf_op jit(solution)/shard_map/ppermute | solution.py:47
  66.0 2.1 %collective-permute-done.1.p1 = bf16[1040,128]{1,0:T(8,128)(2,1)S(1)} collective-permute-done((bf16[1040,128]{1,0:T(8,128)(2,1)S(1)}, bf16[1040,128]{1,0:T(8,128)(2,1)S(1)}, u32[]{:S(2)}, u32[]{:S(2)}) %collective-permute-start.1) | collective-permute-done | bytes 266272 | tf_op jit(solution)/shard_map/ppermute | solution.py:47
  68.0 0.0 copy-done.5
  68.0 0.3 shard_map.116.b0
  68.3 0.1 collective-permute-start.8
  68.4 9.4 %collective-permute-done.8.b1 = bf16[1040,128]{1,0:T(8,128)(2,1)S(1)} collective-permute-done((bf16[1040,128]{1,0:T(8,128)(2,1)S(1)}, bf16[1040,128]{1,0:T(8,128)(2,1)S(1)}, u32[]{:S(2)}, u32[]{:S(2)}) %collective-permute-start.8) | collective-permute-done | bytes 266272 | tf_op jit(solution)/shard_map/ppermute | solution.py:47
  77.8 2.4 %shard_map.119 = (f32[16,400,128]{2,1,0:T(8,128)S(1)}, bf16[16,400,128]{2,1,0:T(8,128)(2,1)S(1)}) custom-call(s32[4]{0:T(128)S(1)} %pad_add_fusion.place_ref, bf16[1040,128]{1,0:T(8,128)(2,1)S(1)} %shard_map.116.b0, bf16[1040,128]{1,0:T(8,128)(2,1)S(1)} %collective-permute-done.8.b1, bf16[1024,512]{1,0:T(8,128)(2,1)S(1)} %get-tuple-element.22.pooled_ref, ...), custom_call_target="tpu_custom_call" | custom-call | flops 2147483648 | bytes 6291456 | tf_op jit(solution)/shard_map/pallas_call | solution.py:59
  80.1 0.1 collective-permute-start.9
  80.2 1.5 %collective-permute-start.4 = (bf16[1040,128]{1,0:T(8,128)(2,1)S(1)}, bf16[1040,128]{1,0:T(8,128)(2,1)S(1)}, u32[]{:S(2)}, u32[]{:S(2)}) collective-permute-start(bf16[1040,128]{1,0:T(8,128)(2,1)S(1)} %shard_map.116.b0), channel_id=1, source_target_pairs={{0,96},{1,33},{2,98},{3,35},{4,100},{5,37},{6,102},{7,39},{8,104},... | collective-permute-start | bytes 798728 | tf_op jit(solution)/shard_map/ppermute | solution.py:47
  81.7 0.6 collective-permute-start.5
  82.3 0.6 shard_map.118
  83.0 1.2 collective-permute-start.7
  84.1 4.9 %collective-permute-done.4.b2 = bf16[1040,128]{1,0:T(8,128)(2,1)S(1)} collective-permute-done((bf16[1040,128]{1,0:T(8,128)(2,1)S(1)}, bf16[1040,128]{1,0:T(8,128)(2,1)S(1)}, u32[]{:S(2)}, u32[]{:S(2)}) %collective-permute-start.4) | collective-permute-done | bytes 266272 | tf_op jit(solution)/shard_map/ppermute | solution.py:47
  89.0 1.2 collective-permute-done.5.b3
  90.2 0.9 shard_map.117
  91.1 0.1 collective-permute-start.6
  91.2 0.5 collective-permute-start.10
  91.7 0.1 collective-permute-start.11
  91.8 0.0 collective-permute-done.7.partner_ref
  91.8 1.7 %collective-permute-done.10.p2 = bf16[1040,128]{1,0:T(8,128)(2,1)S(1)} collective-permute-done((bf16[1040,128]{1,0:T(8,128)(2,1)S(1)}, bf16[1040,128]{1,0:T(8,128)(2,1)S(1)}, u32[]{:S(2)}, u32[]{:S(2)}) %collective-permute-start.10) | collective-permute-done | bytes 266272 | tf_op jit(solution)/shard_map/ppermute | solution.py:47
  93.5 0.4 collective-permute-done.11.p3
  93.9 0.0 collective-permute-done.9.other_ref
  93.9 0.8 shard_map.120.weights_ref
  94.7 0.0 collective-permute-done.6.their_products
  94.7 1.7 %shard_map.121 = bf16[16,400,128]{2,1,0:T(8,128)(2,1)} custom-call(bf16[256,1024]{1,0:T(8,128)(2,1)S(1)} %get-tuple-element.26.own_products, bf16[256,1024]{1,0:T(8,128)(2,1)S(1)} %collective-permute-done.6.their_products, bf16[1536,256]{1,0:T(8,128)(2,1)S(1)} %get-tuple-element.27.own_ref, bf16[1536,256]{1,0:T(8,128)(2,1)S(1)} %collective-permute-done.7.partner_ref, ...), custom_call_target="tpu_custom_call" | custom-call | flops 536870912 | bytes 4194304 | tf_op jit(solution)/shard_map/pallas_call | solution.py:59
  96.5 3.7 %all-to-all-start.1 = ((bf16[16,400,128]{2,1,0:T(8,128)(2,1)}), bf16[16,400,128]{2,1,0:T(8,128)(2,1)S(1)}, u32[]{:S(2)}, u32[]{:S(2)}) async-start(bf16[16,400,128]{2,1,0:T(8,128)(2,1)} %shard_map.121), calls=%async_computation.1 | async-start | bytes 3276800 | tf_op jit(solution)/shard_map/all_to_all | solution.py:485
  100.2 0.0 copy-start.1
  100.2 2.2 %copy-done.1 = bf16[512,4096]{1,0:T(8,128)(2,1)S(1)} copy-done((bf16[512,4096]{1,0:T(8,128)(2,1)S(1)}, bf16[512,4096]{1,0:T(8,128)(2,1)}, u32[]{:S(2)}) %copy-start.1) | copy-done | bytes 4194328
  102.4 0.7 shard_map.122
  103.1 23.9 %all-to-all-done.1.in_ref = bf16[16,400,128]{2,1,0:T(8,128)(2,1)S(1)} async-done(((bf16[16,400,128]{2,1,0:T(8,128)(2,1)}), bf16[16,400,128]{2,1,0:T(8,128)(2,1)S(1)}, u32[]{:S(2)}, u32[]{:S(2)}) %all-to-all-start.1) | async-done | bytes 1638432 | tf_op jit(solution)/shard_map/all_to_all | solution.py:485
  127.0 0.9 shard_map.123
  (1 shorter events, 0.0 us)
Async XLA Ops:
  0.7 45.0 %copy-start.2 = (bf16[4096,512]{1,0:T(8,128)(2,1)S(1)}, bf16[4096,512]{1,0:T(8,128)(2,1)}, u32[]{:S(2)}) copy-start(bf16[4096,512]{1,0:T(8,128)(2,1)} %down_ref.1) | copy-start | bytes 12582916
  3.9 41.8 %copy-start = (bf16[512,4096]{1,0:T(8,128)(2,1)S(1)}, bf16[512,4096]{1,0:T(8,128)(2,1)}, u32[]{:S(2)}) copy-start(bf16[512,4096]{1,0:T(8,128)(2,1)} %up_ref.3) | copy-start | bytes 12582916
  3.9 41.8 %copy-start.3 = (f32[4096]{0:T(1024)S(1)}, f32[4096]{0:T(1024)}, u32[]{:S(2)}) copy-start(f32[4096]{0:T(1024)} %param.12) | copy-start | bytes 49156
  3.9 41.8 %copy-start.4 = (f32[4096]{0:T(1024)S(1)}, f32[4096]{0:T(1024)}, u32[]{:S(2)}) copy-start(f32[4096]{0:T(1024)} %param.11) | copy-start | bytes 49156
  45.5 2.0 %collective-permute-start = (bf16[2048,128]{1,0:T(8,128)(2,1)S(1)}, bf16[2048,128]{1,0:T(8,128)(2,1)S(1)}, u32[]{:S(2)}, u32[]{:S(2)}) collective-permute-start(bf16[2048,128]{1,0:T(8,128)(2,1)S(1)} %slice.4), channel_id=1, source_target_pairs={{0,1},{1,0},{2,3},{3,2},{4,5},{5,4},{6,7},{7,6},{8,9},{9,8},{10,11... | collective-permute-start | bytes 1572872 | tf_op jit(solution)/shard_map/ppermute | solution.py:47
  50.1 18.0 %copy-start.5 = (s32[128]{0:T(128)S(1)}, s32[128]{0:T(128)}, u32[]{:S(2)}) copy-start(s32[128]{0:T(128)} %param.13) | copy-start | bytes 1540
  50.1 9.1 %collective-permute-start.2 = (bf16[1040,128]{1,0:T(8,128)(2,1)S(1)}, bf16[1040,128]{1,0:T(8,128)(2,1)S(1)}, u32[]{:S(2)}, u32[]{:S(2)}) collective-permute-start(bf16[1040,128]{1,0:T(8,128)(2,1)S(1)} %get-tuple-element.24), channel_id=1, source_target_pairs={{0,32},{1,97},{2,34},{3,99},{4,36},{5,101},{6,38},{7,103},{8,40},{... | collective-permute-start | bytes 798728 | tf_op jit(solution)/shard_map/ppermute | solution.py:47
  52.1 13.9 %collective-permute-start.3 = (bf16[1040,128]{1,0:T(8,128)(2,1)S(1)}, bf16[1040,128]{1,0:T(8,128)(2,1)S(1)}, u32[]{:S(2)}, u32[]{:S(2)}) collective-permute-start(bf16[1040,128]{1,0:T(8,128)(2,1)S(1)} %get-tuple-element.25), channel_id=1, source_target_pairs={{0,96},{1,33},{2,98},{3,35},{4,100},{5,37},{6,102},{7,39},{8,104},... | collective-permute-start | bytes 798728 | tf_op jit(solution)/shard_map/ppermute | solution.py:47
  54.3 13.8 %collective-permute-start.1 = (bf16[1040,128]{1,0:T(8,128)(2,1)S(1)}, bf16[1040,128]{1,0:T(8,128)(2,1)S(1)}, u32[]{:S(2)}, u32[]{:S(2)}) collective-permute-start(bf16[1040,128]{1,0:T(8,128)(2,1)S(1)} %get-tuple-element.23), channel_id=1, source_target_pairs={{0,64},{1,65},{2,66},{3,67},{4,68},{5,69},{6,70},{7,71},{8,72},{9,... | collective-permute-start | bytes 798728 | tf_op jit(solution)/shard_map/ppermute | solution.py:47
  68.3 9.4 %collective-permute-start.8 = (bf16[1040,128]{1,0:T(8,128)(2,1)S(1)}, bf16[1040,128]{1,0:T(8,128)(2,1)S(1)}, u32[]{:S(2)}, u32[]{:S(2)}) collective-permute-start(bf16[1040,128]{1,0:T(8,128)(2,1)S(1)} %shard_map.116.b0), channel_id=1, source_target_pairs={{0,64},{1,65},{2,66},{3,67},{4,68},{5,69},{6,70},{7,71},{8,72},{9,... | collective-permute-start | bytes 798728 | tf_op jit(solution)/shard_map/ppermute | solution.py:47
  80.1 13.8 %collective-permute-start.9 = (bf16[16,400,128]{2,1,0:T(8,128)(2,1)S(1)}, bf16[16,400,128]{2,1,0:T(8,128)(2,1)S(1)}, u32[]{:S(2)}, u32[]{:S(2)}) collective-permute-start(bf16[16,400,128]{2,1,0:T(8,128)(2,1)S(1)} %get-tuple-element.30), channel_id=1, source_target_pairs={{0,1},{1,0},{2,3},{3,2},{4,5},{5,4},{6,7},{7,6},{8,9},{9,8},{10,11... | collective-permute-start | bytes 4915208 | tf_op jit(solution)/shard_map/ppermute | solution.py:47
  80.2 8.8 %collective-permute-start.4 = (bf16[1040,128]{1,0:T(8,128)(2,1)S(1)}, bf16[1040,128]{1,0:T(8,128)(2,1)S(1)}, u32[]{:S(2)}, u32[]{:S(2)}) collective-permute-start(bf16[1040,128]{1,0:T(8,128)(2,1)S(1)} %shard_map.116.b0), channel_id=1, source_target_pairs={{0,96},{1,33},{2,98},{3,35},{4,100},{5,37},{6,102},{7,39},{8,104},... | collective-permute-start | bytes 798728 | tf_op jit(solution)/shard_map/ppermute | solution.py:47
  81.7 8.5 %collective-permute-start.5 = (bf16[1040,128]{1,0:T(8,128)(2,1)S(1)}, bf16[1040,128]{1,0:T(8,128)(2,1)S(1)}, u32[]{:S(2)}, u32[]{:S(2)}) collective-permute-start(bf16[1040,128]{1,0:T(8,128)(2,1)S(1)} %shard_map.116.b0), channel_id=1, source_target_pairs={{0,32},{1,97},{2,34},{3,99},{4,36},{5,101},{6,38},{7,103},{8,40},{... | collective-permute-start | bytes 798728 | tf_op jit(solution)/shard_map/ppermute | solution.py:47
  83.0 8.8 %collective-permute-start.7 = (bf16[1536,256]{1,0:T(8,128)(2,1)S(1)}, bf16[1536,256]{1,0:T(8,128)(2,1)S(1)}, u32[]{:S(2)}, u32[]{:S(2)}) collective-permute-start(bf16[1536,256]{1,0:T(8,128)(2,1)S(1)} %get-tuple-element.28), channel_id=1, source_target_pairs={{0,1},{1,0},{2,3},{3,2},{4,5},{5,4},{6,7},{7,6},{8,9},{9,8},{10,11... | collective-permute-start | bytes 2359304 | tf_op jit(solution)/shard_map/ppermute | solution.py:47
  91.1 3.6 %collective-permute-start.6 = (bf16[256,1024]{1,0:T(8,128)(2,1)S(1)}, bf16[256,1024]{1,0:T(8,128)(2,1)S(1)}, u32[]{:S(2)}, u32[]{:S(2)}) collective-permute-start(bf16[256,1024]{1,0:T(8,128)(2,1)S(1)} %get-tuple-element.26.own_products), channel_id=1, source_target_pairs={{0,1},{1,0},{2,3},{3,2},{4,5},{5,4},{6,7},{7,6},{8,9},{9,8},{10,11... | collective-permute-start | bytes 1572872 | tf_op jit(solution)/shard_map/ppermute | solution.py:47
  91.2 2.3 %collective-permute-start.10 = (bf16[1040,128]{1,0:T(8,128)(2,1)S(1)}, bf16[1040,128]{1,0:T(8,128)(2,1)S(1)}, u32[]{:S(2)}, u32[]{:S(2)}) collective-permute-start(bf16[1040,128]{1,0:T(8,128)(2,1)S(1)} %collective-permute-done.4.b2), channel_id=1, source_target_pairs={{0,1},{1,0},{2,3},{3,2},{4,5},{5,4},{6,7},{7,6},{8,9},{9,8},{10,11... | collective-permute-start | bytes 798728 | tf_op jit(solution)/shard_map/ppermute | solution.py:47
  91.7 2.2 %collective-permute-start.11 = (bf16[1040,128]{1,0:T(8,128)(2,1)S(1)}, bf16[1040,128]{1,0:T(8,128)(2,1)S(1)}, u32[]{:S(2)}, u32[]{:S(2)}) collective-permute-start(bf16[1040,128]{1,0:T(8,128)(2,1)S(1)} %collective-permute-done.5.b3), channel_id=1, source_target_pairs={{0,1},{1,0},{2,3},{3,2},{4,5},{5,4},{6,7},{7,6},{8,9},{9,8},{10,11... | collective-permute-start | bytes 798728 | tf_op jit(solution)/shard_map/ppermute | solution.py:47
  96.5 30.5 %all-to-all-start.1 = ((bf16[16,400,128]{2,1,0:T(8,128)(2,1)}), bf16[16,400,128]{2,1,0:T(8,128)(2,1)S(1)}, u32[]{:S(2)}, u32[]{:S(2)}) async-start(bf16[16,400,128]{2,1,0:T(8,128)(2,1)} %shard_map.121), calls=%async_computation.1 | async-start | bytes 3276800 | tf_op jit(solution)/shard_map/all_to_all | solution.py:485
  100.2 2.2 %copy-start.1 = (bf16[512,4096]{1,0:T(8,128)(2,1)S(1)}, bf16[512,4096]{1,0:T(8,128)(2,1)}, u32[]{:S(2)}) copy-start(bf16[512,4096]{1,0:T(8,128)(2,1)} %up_ref.3) | copy-start | bytes 12582916

commit v2 on v1

--- a/solution.py
+++ b/solution.py
@@ -204,7 +204,7 @@
             pooled_ref[pl.ds(partners, HALF), :] = dot(
                 other_ref[at, :].T, in_ref[at, :SAMPLES], 1, 0
             ).astype(BF16)
-        products(rows_ref, pooled_ref[:, OWN : 2 * OWN], (out,))
+        products(rows_ref, pooled_ref[:, 2 * OWN : 3 * OWN], (out,))
 
     return call(
         body,
@@ -217,7 +217,8 @@
 
 def forward_near(pooled, rows):
     def body(pooled_ref, rows_ref, *outs):
-        products(rows_ref, pooled_ref[:, 2 * OWN :], outs)
+        ends = [pooled_ref[:, OWN : 2 * OWN], pooled_ref[:, 3 * OWN :]]
+        products(rows_ref, jnp.concatenate(ends, axis=1), outs)
 
     return call(
         body,
@@ -459,10 +460,10 @@
     arrived = lax.all_to_all(sent, PLANE, 0, 0, tiled=True).reshape(PEERS * ROWS, SAMPLES + HALF)
     other = shift(arrived[:, SAMPLES:], dc=1)
     half = pool_half(arrived)
-    pooled, chunk1 = forward_far(place, arrived, other, half, rows)
+    pooled, chunk2 = forward_far(place, arrived, other, half, rows)
+    part2 = shift(chunk2, dz=(ORDER[0][2], ORDER[1][2]))
+    chunk1, chunk3 = forward_near(pooled, rows)
     part1 = shift(chunk1, dz=(ORDER[0][1], ORDER[1][1]))
-    chunk2, chunk3 = forward_near(pooled, rows)
-    part2 = shift(chunk2, dz=(ORDER[0][2], ORDER[1][2]))
     part3 = shift(chunk3, dz=(ORDER[0][3], ORDER[1][3]))
     parts = [part1, part2, part3]
     chunk = forward_own(pooled, rows)

time: 128 us -> 128 us (level)
  starting transfers between devices: 14 us -> 16.3 us
  waiting for transfers between devices: 52.8 us -> 50.6 us
    ppermute x12, starting transfers between devices: 10.3 us -> 12.6 us  [shift(): return lax.ppermute(value, ALL, pairs)]
    ppermute x12, waiting for transfers between devices: 28.9 us -> 26.7 us  [shift(): return lax.ppermute(value, ALL, pairs)]
  transfers between devices with their start and end apart: 13 -> 13, of which waited for: 10 -> 9; matrix products, arithmetic and copies ran while one was open for 0% -> 0% of each run, Pallas kernels for 4% -> 4%
where the time goes in v2:
time: 128 us
  waiting for transfers between devices  50.6 us (40%)
  blocking collectives  41.6 us (32%)
  Pallas kernels  16.5 us (13%)
  starting transfers between devices  16.3 us (13%)
  local copies, waits for them, and re-layouts  2.25 us (2%)
    all_to_all x1, blocking collectives, local(): lax.all_to_all(sent, PLANE, 0, 0, tiled=True)  41.6 us
    ppermute x12, waiting for transfers between devices, shift(): return lax.ppermute(value, ALL, pairs)  26.7 us
    all_to_all x1, waiting for transfers between devices, local(): shares = lax.all_to_all(summed, ('y', 'x'), 0, 0, tiled=True)  23.9 us
    pallas_call x14, Pallas kernels, call(): pl.pallas_call(body, in_specs=specs or [pl.BlockSpec(memory_space=pltpu.V...  16.5 us
    ppermute x12, starting transfers between devices, shift(): return lax.ppermute(value, ALL, pairs)  12.6 us
    all_to_all x1, starting transfers between devices, local(): shares = lax.all_to_all(summed, ('y', 'x'), 0, 0, tiled=True)  3.71 us
  transfers between devices with their start and end apart: 13, of which 9 were waited for; matrix products, arithmetic and copies ran while one was open for 0% of the time, Pallas kernels for 4%

profile of v2, /device:TPU:0, one launch (start us, length us, event | category | flops | bytes accessed | tf_op | source)
XLA Modules:
  0.0 128.0 jit_solution(18292699756380375342)
XLA Ops:
  0.6 0.1 pad_add_fusion.place_ref
  0.7 0.0 copy-start.2
  0.7 3.1 %shard_map.110 = bf16[32,64,640]{2,1,0:T(8,128)(2,1)S(1)} custom-call(s32[4]{0:T(128)S(1)} %pad_add_fusion.place_ref, s32[64,16384]{1,0:T(8,128)} %bitcast.22, bf16[64,256]{1,0:T(8,128)(2,1)} %slab_ref.1), custom_call_target="tpu_custom_call" | custom-call | tf_op jit(solution)/shard_map/pallas_call | solution.py:59
  3.9 0.0 copy-start
  3.9 0.0 copy-start.3
  3.9 0.0 copy-start.4
  3.9 41.6 %all_to_all.10 = bf16[32,64,640]{2,1,0:T(8,128)(2,1)S(1)} all-to-all(bf16[32,64,640]{2,1,0:T(8,128)(2,1)S(1)} %shard_map.110), channel_id=1, replica_groups=mesh['z'=4,'y'=4,'x'=4,'c'=2] {'y','x','c'}, dimensions={0} | all-to-all | bytes 5242880 | tf_op jit(solution)/shard_map/all_to_all | solution.py:460
  45.5 0.2 collective-permute-start
  45.7 0.0 copy-done.2
  45.7 0.0 copy-done
  45.7 0.0 copy-done.3
  45.7 0.0 copy-done.4
  45.7 1.2 shard_map.112.rows_ref
  46.9 0.5 shard_map.111.half_ref
  47.3 0.1 collective-permute-done.other_ref
  47.5 1.8 %shard_map.113 = (bf16[1024,512]{1,0:T(8,128)(2,1)S(1)}, bf16[1040,128]{1,0:T(8,128)(2,1)S(1)}) custom-call(s32[4]{0:T(128)S(1)} %pad_add_fusion.place_ref, bf16[2048,640]{1,0:T(8,128)(2,1)S(1)} %bitcast.14, bf16[2048,128]{1,0:T(8,128)(2,1)S(1)} %collective-permute-done.other_ref, bf16[512,512]{1,0:T(8,128)(2,1)S(1)} %shard_map.111.half_ref, ...), custom_call_target="tpu_custom_call" | custom-call | flops 3221225472 | bytes 4194304 | tf_op jit(solution)/shard_map/pallas_call | solution.py:59
  49.3 0.8 shard_map.115
  50.1 0.0 copy-start.5
  50.1 4.0 %collective-permute-start.1 = (bf16[1040,128]{1,0:T(8,128)(2,1)S(1)}, bf16[1040,128]{1,0:T(8,128)(2,1)S(1)}, u32[]{:S(2)}, u32[]{:S(2)}) collective-permute-start(bf16[1040,128]{1,0:T(8,128)(2,1)S(1)} %get-tuple-element.23), channel_id=1, source_target_pairs={{0,64},{1,65},{2,66},{3,67},{4,68},{5,69},{6,70},{7,71},{8,72},{9,... | collective-permute-start | bytes 798728 | tf_op jit(solution)/shard_map/ppermute | solution.py:47
  54.0 0.7 collective-permute-start.3
  54.8 1.3 %collective-permute-start.2 = (bf16[1040,128]{1,0:T(8,128)(2,1)S(1)}, bf16[1040,128]{1,0:T(8,128)(2,1)S(1)}, u32[]{:S(2)}, u32[]{:S(2)}) collective-permute-start(bf16[1040,128]{1,0:T(8,128)(2,1)S(1)} %get-tuple-element.24), channel_id=1, source_target_pairs={{0,32},{1,97},{2,34},{3,99},{4,36},{5,101},{6,38},{7,103},{8,40},{... | collective-permute-start | bytes 798728 | tf_op jit(solution)/shard_map/ppermute | solution.py:47
  56.1 0.7 shard_map.114.p0
  56.8 4.5 %collective-permute-done.1.p1 = bf16[1040,128]{1,0:T(8,128)(2,1)S(1)} collective-permute-done((bf16[1040,128]{1,0:T(8,128)(2,1)S(1)}, bf16[1040,128]{1,0:T(8,128)(2,1)S(1)}, u32[]{:S(2)}, u32[]{:S(2)}) %collective-permute-start.1) | collective-permute-done | bytes 266272 | tf_op jit(solution)/shard_map/ppermute | solution.py:47
  61.3 6.0 %collective-permute-done.3.p3 = bf16[1040,128]{1,0:T(8,128)(2,1)S(1)} collective-permute-done((bf16[1040,128]{1,0:T(8,128)(2,1)S(1)}, bf16[1040,128]{1,0:T(8,128)(2,1)S(1)}, u32[]{:S(2)}, u32[]{:S(2)}) %collective-permute-start.3) | collective-permute-done | bytes 266272 | tf_op jit(solution)/shard_map/ppermute | solution.py:47
  67.4 0.0 collective-permute-done.2.p2
  67.4 0.0 copy-done.5
  67.4 0.3 shard_map.116.b0
  67.6 2.1 %collective-permute-start.8 = (bf16[1040,128]{1,0:T(8,128)(2,1)S(1)}, bf16[1040,128]{1,0:T(8,128)(2,1)S(1)}, u32[]{:S(2)}, u32[]{:S(2)}) collective-permute-start(bf16[1040,128]{1,0:T(8,128)(2,1)S(1)} %shard_map.116.b0), channel_id=1, source_target_pairs={{0,64},{1,65},{2,66},{3,67},{4,68},{5,69},{6,70},{7,71},{8,72},{9,... | collective-permute-start | bytes 798728 | tf_op jit(solution)/shard_map/ppermute | solution.py:47
  69.7 7.2 %collective-permute-done.8.b1 = bf16[1040,128]{1,0:T(8,128)(2,1)S(1)} collective-permute-done((bf16[1040,128]{1,0:T(8,128)(2,1)S(1)}, bf16[1040,128]{1,0:T(8,128)(2,1)S(1)}, u32[]{:S(2)}, u32[]{:S(2)}) %collective-permute-start.8) | collective-permute-done | bytes 266272 | tf_op jit(solution)/shard_map/ppermute | solution.py:47
  76.9 2.4 %shard_map.119 = (f32[16,400,128]{2,1,0:T(8,128)S(1)}, bf16[16,400,128]{2,1,0:T(8,128)(2,1)S(1)}) custom-call(s32[4]{0:T(128)S(1)} %pad_add_fusion.place_ref, bf16[1040,128]{1,0:T(8,128)(2,1)S(1)} %shard_map.116.b0, bf16[1040,128]{1,0:T(8,128)(2,1)S(1)} %collective-permute-done.8.b1, bf16[1024,512]{1,0:T(8,128)(2,1)S(1)} %get-tuple-element.22.pooled_ref, ...), custom_call_target="tpu_custom_call" | custom-call | flops 2147483648 | bytes 6291456 | tf_op jit(solution)/shard_map/pallas_call | solution.py:59
  79.3 0.1 collective-permute-start.9
  79.4 3.3 %collective-permute-start.4 = (bf16[1040,128]{1,0:T(8,128)(2,1)S(1)}, bf16[1040,128]{1,0:T(8,128)(2,1)S(1)}, u32[]{:S(2)}, u32[]{:S(2)}) collective-permute-start(bf16[1040,128]{1,0:T(8,128)(2,1)S(1)} %shard_map.116.b0), channel_id=1, source_target_pairs={{0,96},{1,33},{2,98},{3,35},{4,100},{5,37},{6,102},{7,39},{8,104},... | collective-permute-start | bytes 798728 | tf_op jit(solution)/shard_map/ppermute | solution.py:47
  82.7 0.0 collective-permute-start.5
  82.7 0.6 shard_map.118
  83.4 0.2 collective-permute-start.7
  83.6 5.4 %collective-permute-done.4.b2 = bf16[1040,128]{1,0:T(8,128)(2,1)S(1)} collective-permute-done((bf16[1040,128]{1,0:T(8,128)(2,1)S(1)}, bf16[1040,128]{1,0:T(8,128)(2,1)S(1)}, u32[]{:S(2)}, u32[]{:S(2)}) %collective-permute-start.4) | collective-permute-done | bytes 266272 | tf_op jit(solution)/shard_map/ppermute | solution.py:47
  89.0 1.4 %collective-permute-done.5.b3 = bf16[1040,128]{1,0:T(8,128)(2,1)S(1)} collective-permute-done((bf16[1040,128]{1,0:T(8,128)(2,1)S(1)}, bf16[1040,128]{1,0:T(8,128)(2,1)S(1)}, u32[]{:S(2)}, u32[]{:S(2)}) %collective-permute-start.5) | collective-permute-done | bytes 266272 | tf_op jit(solution)/shard_map/ppermute | solution.py:47
  90.3 0.9 shard_map.117
  91.2 0.1 collective-permute-start.6
  91.3 0.5 collective-permute-start.10
  91.8 0.1 collective-permute-start.11
  91.9 0.0 collective-permute-done.7.partner_ref
  91.9 1.7 %collective-permute-done.10.p2 = bf16[1040,128]{1,0:T(8,128)(2,1)S(1)} collective-permute-done((bf16[1040,128]{1,0:T(8,128)(2,1)S(1)}, bf16[1040,128]{1,0:T(8,128)(2,1)S(1)}, u32[]{:S(2)}, u32[]{:S(2)}) %collective-permute-start.10) | collective-permute-done | bytes 266272 | tf_op jit(solution)/shard_map/ppermute | solution.py:47
  93.6 0.4 collective-permute-done.11.p3
  94.0 0.0 collective-permute-done.9.other_ref
  94.0 0.8 shard_map.120.weights_ref
  94.8 0.0 collective-permute-done.6.their_products
  94.8 1.7 %shard_map.121 = bf16[16,400,128]{2,1,0:T(8,128)(2,1)} custom-call(bf16[256,1024]{1,0:T(8,128)(2,1)S(1)} %get-tuple-element.26.own_products, bf16[256,1024]{1,0:T(8,128)(2,1)S(1)} %collective-permute-done.6.their_products, bf16[1536,256]{1,0:T(8,128)(2,1)S(1)} %get-tuple-element.27.own_ref, bf16[1536,256]{1,0:T(8,128)(2,1)S(1)} %collective-permute-done.7.partner_ref, ...), custom_call_target="tpu_custom_call" | custom-call | flops 536870912 | bytes 4194304 | tf_op jit(solution)/shard_map/pallas_call | solution.py:59
  96.6 3.7 %all-to-all-start.1 = ((bf16[16,400,128]{2,1,0:T(8,128)(2,1)}), bf16[16,400,128]{2,1,0:T(8,128)(2,1)S(1)}, u32[]{:S(2)}, u32[]{:S(2)}) async-start(bf16[16,400,128]{2,1,0:T(8,128)(2,1)} %shard_map.121), calls=%async_computation.1 | async-start | bytes 3276800 | tf_op jit(solution)/shard_map/all_to_all | solution.py:486
  100.3 0.0 copy-start.1
  100.3 2.2 %copy-done.1 = bf16[512,4096]{1,0:T(8,128)(2,1)S(1)} copy-done((bf16[512,4096]{1,0:T(8,128)(2,1)S(1)}, bf16[512,4096]{1,0:T(8,128)(2,1)}, u32[]{:S(2)}) %copy-start.1) | copy-done | bytes 4194328
  102.5 0.7 shard_map.122
  103.2 23.9 %all-to-all-done.1.in_ref = bf16[16,400,128]{2,1,0:T(8,128)(2,1)S(1)} async-done(((bf16[16,400,128]{2,1,0:T(8,128)(2,1)}), bf16[16,400,128]{2,1,0:T(8,128)(2,1)S(1)}, u32[]{:S(2)}, u32[]{:S(2)}) %all-to-all-start.1) | async-done | bytes 1638432 | tf_op jit(solution)/shard_map/all_to_all | solution.py:486
  127.1 0.9 shard_map.123
  (1 shorter events, 0.0 us)
Async XLA Ops:
  0.7 45.0 %copy-start.2 = (bf16[4096,512]{1,0:T(8,128)(2,1)S(1)}, bf16[4096,512]{1,0:T(8,128)(2,1)}, u32[]{:S(2)}) copy-start(bf16[4096,512]{1,0:T(8,128)(2,1)} %down_ref.1) | copy-start | bytes 12582916
  3.9 41.8 %copy-start = (bf16[512,4096]{1,0:T(8,128)(2,1)S(1)}, bf16[512,4096]{1,0:T(8,128)(2,1)}, u32[]{:S(2)}) copy-start(bf16[512,4096]{1,0:T(8,128)(2,1)} %up_ref.3) | copy-start | bytes 12582916
  3.9 41.8 %copy-start.3 = (f32[4096]{0:T(1024)S(1)}, f32[4096]{0:T(1024)}, u32[]{:S(2)}) copy-start(f32[4096]{0:T(1024)} %param.12) | copy-start | bytes 49156
  3.9 41.8 %copy-start.4 = (f32[4096]{0:T(1024)S(1)}, f32[4096]{0:T(1024)}, u32[]{:S(2)}) copy-start(f32[4096]{0:T(1024)} %param.11) | copy-start | bytes 49156
  45.5 2.0 %collective-permute-start = (bf16[2048,128]{1,0:T(8,128)(2,1)S(1)}, bf16[2048,128]{1,0:T(8,128)(2,1)S(1)}, u32[]{:S(2)}, u32[]{:S(2)}) collective-permute-start(bf16[2048,128]{1,0:T(8,128)(2,1)S(1)} %slice.4), channel_id=1, source_target_pairs={{0,1},{1,0},{2,3},{3,2},{4,5},{5,4},{6,7},{7,6},{8,9},{9,8},{10,11... | collective-permute-start | bytes 1572872 | tf_op jit(solution)/shard_map/ppermute | solution.py:47
  50.1 17.3 %copy-start.5 = (s32[128]{0:T(128)S(1)}, s32[128]{0:T(128)}, u32[]{:S(2)}) copy-start(s32[128]{0:T(128)} %param.13) | copy-start | bytes 1540
  50.1 11.2 %collective-permute-start.1 = (bf16[1040,128]{1,0:T(8,128)(2,1)S(1)}, bf16[1040,128]{1,0:T(8,128)(2,1)S(1)}, u32[]{:S(2)}, u32[]{:S(2)}) collective-permute-start(bf16[1040,128]{1,0:T(8,128)(2,1)S(1)} %get-tuple-element.23), channel_id=1, source_target_pairs={{0,64},{1,65},{2,66},{3,67},{4,68},{5,69},{6,70},{7,71},{8,72},{9,... | collective-permute-start | bytes 798728 | tf_op jit(solution)/shard_map/ppermute | solution.py:47
  54.0 13.3 %collective-permute-start.3 = (bf16[1040,128]{1,0:T(8,128)(2,1)S(1)}, bf16[1040,128]{1,0:T(8,128)(2,1)S(1)}, u32[]{:S(2)}, u32[]{:S(2)}) collective-permute-start(bf16[1040,128]{1,0:T(8,128)(2,1)S(1)} %get-tuple-element.25), channel_id=1, source_target_pairs={{0,96},{1,33},{2,98},{3,35},{4,100},{5,37},{6,102},{7,39},{8,104},... | collective-permute-start | bytes 798728 | tf_op jit(solution)/shard_map/ppermute | solution.py:47
  54.8 12.6 %collective-permute-start.2 = (bf16[1040,128]{1,0:T(8,128)(2,1)S(1)}, bf16[1040,128]{1,0:T(8,128)(2,1)S(1)}, u32[]{:S(2)}, u32[]{:S(2)}) collective-permute-start(bf16[1040,128]{1,0:T(8,128)(2,1)S(1)} %get-tuple-element.24), channel_id=1, source_target_pairs={{0,32},{1,97},{2,34},{3,99},{4,36},{5,101},{6,38},{7,103},{8,40},{... | collective-permute-start | bytes 798728 | tf_op jit(solution)/shard_map/ppermute | solution.py:47
  67.6 9.3 %collective-permute-start.8 = (bf16[1040,128]{1,0:T(8,128)(2,1)S(1)}, bf16[1040,128]{1,0:T(8,128)(2,1)S(1)}, u32[]{:S(2)}, u32[]{:S(2)}) collective-permute-start(bf16[1040,128]{1,0:T(8,128)(2,1)S(1)} %shard_map.116.b0), channel_id=1, source_target_pairs={{0,64},{1,65},{2,66},{3,67},{4,68},{5,69},{6,70},{7,71},{8,72},{9,... | collective-permute-start | bytes 798728 | tf_op jit(solution)/shard_map/ppermute | solution.py:47
  79.3 14.7 %collective-permute-start.9 = (bf16[16,400,128]{2,1,0:T(8,128)(2,1)S(1)}, bf16[16,400,128]{2,1,0:T(8,128)(2,1)S(1)}, u32[]{:S(2)}, u32[]{:S(2)}) collective-permute-start(bf16[16,400,128]{2,1,0:T(8,128)(2,1)S(1)} %get-tuple-element.30), channel_id=1, source_target_pairs={{0,1},{1,0},{2,3},{3,2},{4,5},{5,4},{6,7},{7,6},{8,9},{9,8},{10,11... | collective-permute-start | bytes 4915208 | tf_op jit(solution)/shard_map/ppermute | solution.py:47
  79.4 9.5 %collective-permute-start.4 = (bf16[1040,128]{1,0:T(8,128)(2,1)S(1)}, bf16[1040,128]{1,0:T(8,128)(2,1)S(1)}, u32[]{:S(2)}, u32[]{:S(2)}) collective-permute-start(bf16[1040,128]{1,0:T(8,128)(2,1)S(1)} %shard_map.116.b0), channel_id=1, source_target_pairs={{0,96},{1,33},{2,98},{3,35},{4,100},{5,37},{6,102},{7,39},{8,104},... | collective-permute-start | bytes 798728 | tf_op jit(solution)/shard_map/ppermute | solution.py:47
  82.7 7.6 %collective-permute-start.5 = (bf16[1040,128]{1,0:T(8,128)(2,1)S(1)}, bf16[1040,128]{1,0:T(8,128)(2,1)S(1)}, u32[]{:S(2)}, u32[]{:S(2)}) collective-permute-start(bf16[1040,128]{1,0:T(8,128)(2,1)S(1)} %shard_map.116.b0), channel_id=1, source_target_pairs={{0,32},{1,97},{2,34},{3,99},{4,36},{5,101},{6,38},{7,103},{8,40},{... | collective-permute-start | bytes 798728 | tf_op jit(solution)/shard_map/ppermute | solution.py:47
  83.4 8.5 %collective-permute-start.7 = (bf16[1536,256]{1,0:T(8,128)(2,1)S(1)}, bf16[1536,256]{1,0:T(8,128)(2,1)S(1)}, u32[]{:S(2)}, u32[]{:S(2)}) collective-permute-start(bf16[1536,256]{1,0:T(8,128)(2,1)S(1)} %get-tuple-element.28), channel_id=1, source_target_pairs={{0,1},{1,0},{2,3},{3,2},{4,5},{5,4},{6,7},{7,6},{8,9},{9,8},{10,11... | collective-permute-start | bytes 2359304 | tf_op jit(solution)/shard_map/ppermute | solution.py:47
  91.2 3.6 %collective-permute-start.6 = (bf16[256,1024]{1,0:T(8,128)(2,1)S(1)}, bf16[256,1024]{1,0:T(8,128)(2,1)S(1)}, u32[]{:S(2)}, u32[]{:S(2)}) collective-permute-start(bf16[256,1024]{1,0:T(8,128)(2,1)S(1)} %get-tuple-element.26.own_products), channel_id=1, source_target_pairs={{0,1},{1,0},{2,3},{3,2},{4,5},{5,4},{6,7},{7,6},{8,9},{9,8},{10,11... | collective-permute-start | bytes 1572872 | tf_op jit(solution)/shard_map/ppermute | solution.py:47
  91.3 2.3 %collective-permute-start.10 = (bf16[1040,128]{1,0:T(8,128)(2,1)S(1)}, bf16[1040,128]{1,0:T(8,128)(2,1)S(1)}, u32[]{:S(2)}, u32[]{:S(2)}) collective-permute-start(bf16[1040,128]{1,0:T(8,128)(2,1)S(1)} %collective-permute-done.4.b2), channel_id=1, source_target_pairs={{0,1},{1,0},{2,3},{3,2},{4,5},{5,4},{6,7},{7,6},{8,9},{9,8},{10,11... | collective-permute-start | bytes 798728 | tf_op jit(solution)/shard_map/ppermute | solution.py:47
  91.8 2.2 %collective-permute-start.11 = (bf16[1040,128]{1,0:T(8,128)(2,1)S(1)}, bf16[1040,128]{1,0:T(8,128)(2,1)S(1)}, u32[]{:S(2)}, u32[]{:S(2)}) collective-permute-start(bf16[1040,128]{1,0:T(8,128)(2,1)S(1)} %collective-permute-done.5.b3), channel_id=1, source_target_pairs={{0,1},{1,0},{2,3},{3,2},{4,5},{5,4},{6,7},{7,6},{8,9},{9,8},{10,11... | collective-permute-start | bytes 798728 | tf_op jit(solution)/shard_map/ppermute | solution.py:47
  96.6 30.5 %all-to-all-start.1 = ((bf16[16,400,128]{2,1,0:T(8,128)(2,1)}), bf16[16,400,128]{2,1,0:T(8,128)(2,1)S(1)}, u32[]{:S(2)}, u32[]{:S(2)}) async-start(bf16[16,400,128]{2,1,0:T(8,128)(2,1)} %shard_map.121), calls=%async_computation.1 | async-start | bytes 3276800 | tf_op jit(solution)/shard_map/all_to_all | solution.py:486
  100.3 2.2 %copy-start.1 = (bf16[512,4096]{1,0:T(8,128)(2,1)S(1)}, bf16[512,4096]{1,0:T(8,128)(2,1)}, u32[]{:S(2)}) copy-start(bf16[512,4096]{1,0:T(8,128)(2,1)} %up_ref.3) | copy-start | bytes 12582916

commit v3 on v2

--- a/solution.py
+++ b/solution.py
@@ -194,7 +194,7 @@
 
 
 def forward_far(place, arrived, other, half, rows):
-    def body(place_ref, in_ref, other_ref, half_ref, rows_ref, pooled_ref, out):
+    def body(place_ref, in_ref, other_ref, half_ref, rows_ref, pooled_ref, *outs):
         core = place_ref[3]
         for y in range(NY):
             at = slice(y * 512, (y + 1) * 512)
@@ -204,11 +204,11 @@
             pooled_ref[pl.ds(partners, HALF), :] = dot(
                 other_ref[at, :].T, in_ref[at, :SAMPLES], 1, 0
             ).astype(BF16)
-        products(rows_ref, pooled_ref[:, 2 * OWN : 3 * OWN], (out,))
-
-    return call(
-        body,
-        [pltpu.VMEM((COLS, SAMPLES), BF16), pltpu.VMEM((2 * RANK + EXT, OWN), BF16)],
+        products(rows_ref, pooled_ref[:, OWN : 3 * OWN], outs)
+
+    return call(
+        body,
+        [pltpu.VMEM((COLS, SAMPLES), BF16)] + [pltpu.VMEM((2 * RANK + EXT, OWN), BF16)] * 2,
         (place, near(arrived), near(other), near(half), near(rows)),
         [IN_SMEM] + [IN_VMEM] * 4,
         cost=pl.CostEstimate(flops=3 << 30, bytes_accessed=4 << 20, transcendentals=0),
@@ -216,16 +216,15 @@
 
 
 def forward_near(pooled, rows):
-    def body(pooled_ref, rows_ref, *outs):
-        ends = [pooled_ref[:, OWN : 2 * OWN], pooled_ref[:, 3 * OWN :]]
-        products(rows_ref, jnp.concatenate(ends, axis=1), outs)
-
-    return call(
-        body,
-        [pltpu.VMEM((2 * RANK + EXT, OWN), BF16)] * 2,
+    def body(pooled_ref, rows_ref, out):
+        products(rows_ref, pooled_ref[:, 3 * OWN :], (out,))
+
+    return call(
+        body,
+        [pltpu.VMEM((2 * RANK + EXT, OWN), BF16)],
         (near(pooled), near(rows)),
         cost=pl.CostEstimate(flops=1 << 30, bytes_accessed=2 << 20, transcendentals=0),
-    )
+    )[0]
 
 
 def forward_own(pooled, rows):
@@ -460,10 +459,10 @@
     arrived = lax.all_to_all(sent, PLANE, 0, 0, tiled=True).reshape(PEERS * ROWS, SAMPLES + HALF)
     other = shift(arrived[:, SAMPLES:], dc=1)
     half = pool_half(arrived)
-    pooled, chunk2 = forward_far(place, arrived, other, half, rows)
+    pooled, chunk1, chunk2 = forward_far(place, arrived, other, half, rows)
     part2 = shift(chunk2, dz=(ORDER[0][2], ORDER[1][2]))
-    chunk1, chunk3 = forward_near(pooled, rows)
     part1 = shift(chunk1, dz=(ORDER[0][1], ORDER[1][1]))
+    chunk3 = forward_near(pooled, rows)
     part3 = shift(chunk3, dz=(ORDER[0][3], ORDER[1][3]))
     parts = [part1, part2, part3]
     chunk = forward_own(pooled, rows)

time: 128 us -> 128 us (level)
  starting transfers between devices: 16.3 us -> 14.6 us
  waiting for transfers between devices: 50.6 us -> 52.3 us
    ppermute x12, waiting for transfers between devices: 26.7 us -> 28.4 us  [shift(): return lax.ppermute(value, ALL, pairs)]
    ppermute x12, starting transfers between devices: 12.6 us -> 10.9 us  [shift(): return lax.ppermute(value, ALL, pairs)]
where the time goes in v3:
time: 128 us
  waiting for transfers between devices  52.3 us (41%)
  blocking collectives  41.6 us (32%)
  Pallas kernels  16.4 us (13%)
  starting transfers between devices  14.6 us (11%)
  local copies, waits for them, and re-layouts  2.24 us (2%)
    all_to_all x1, blocking collectives, local(): lax.all_to_all(sent, PLANE, 0, 0, tiled=True)  41.6 us
    ppermute x12, waiting for transfers between devices, shift(): return lax.ppermute(value, ALL, pairs)  28.4 us
    all_to_all x1, waiting for transfers between devices, local(): shares = lax.all_to_all(summed, ('y', 'x'), 0, 0, tiled=True)  23.9 us
    pallas_call x14, Pallas kernels, call(): pl.pallas_call(body, in_specs=specs or [pl.BlockSpec(memory_space=pltpu.V...  16.4 us
    ppermute x12, starting transfers between devices, shift(): return lax.ppermute(value, ALL, pairs)  10.9 us
    all_to_all x1, starting transfers between devices, local(): shares = lax.all_to_all(summed, ('y', 'x'), 0, 0, tiled=True)  3.71 us
  transfers between devices with their start and end apart: 13, of which 9 were waited for; matrix products, arithmetic and copies ran while one was open for 0% of the time, Pallas kernels for 4%

profile of v3, /device:TPU:0, one launch (start us, length us, event | category | flops | bytes accessed | tf_op | source)
XLA Modules:
  0.0 128.0 jit_solution(15067328098990699663)
XLA Ops:
  0.6 0.1 pad_add_fusion.place_ref
  0.7 0.0 copy-start.2
  0.7 3.1 %shard_map.110 = bf16[32,64,640]{2,1,0:T(8,128)(2,1)S(1)} custom-call(s32[4]{0:T(128)S(1)} %pad_add_fusion.place_ref, s32[64,16384]{1,0:T(8,128)} %bitcast.22, bf16[64,256]{1,0:T(8,128)(2,1)} %slab_ref.1), custom_call_target="tpu_custom_call" | custom-call | tf_op jit(solution)/shard_map/pallas_call | solution.py:59
  3.9 0.0 copy-start
  3.9 0.0 copy-start.3
  3.9 0.0 copy-start.4
  3.9 41.6 %all_to_all.10 = bf16[32,64,640]{2,1,0:T(8,128)(2,1)S(1)} all-to-all(bf16[32,64,640]{2,1,0:T(8,128)(2,1)S(1)} %shard_map.110), channel_id=1, replica_groups=mesh['z'=4,'y'=4,'x'=4,'c'=2] {'y','x','c'}, dimensions={0} | all-to-all | bytes 5242880 | tf_op jit(solution)/shard_map/all_to_all | solution.py:459
  45.5 0.2 collective-permute-start
  45.7 0.0 copy-done.2
  45.7 0.0 copy-done
  45.7 0.0 copy-done.3
  45.7 0.0 copy-done.4
  45.7 1.2 shard_map.112.rows_ref
  46.9 0.5 shard_map.111.half_ref
  47.3 0.1 collective-permute-done.other_ref
  47.5 1.8 %shard_map.113 = (bf16[1024,512]{1,0:T(8,128)(2,1)S(1)}, bf16[1040,128]{1,0:T(8,128)(2,1)S(1)}, bf16[1040,128]{1,0:T(8,128)(2,1)S(1)}) custom-call(s32[4]{0:T(128)S(1)} %pad_add_fusion.place_ref, bf16[2048,640]{1,0:T(8,128)(2,1)S(1)} %bitcast.14, bf16[2048,128]{1,0:T(8,128)(2,1)S(1)} %collective-permute-done.other_ref, ...), custom_call_target="tpu_custom_call" | custom-call | flops 3221225472 | bytes 4194304 | tf_op jit(solution)/shard_map/pallas_call | solution.py:59
  49.3 0.7 shard_map.115
  50.0 0.0 copy-start.5
  50.0 4.1 %collective-permute-start.3 = (bf16[1040,128]{1,0:T(8,128)(2,1)S(1)}, bf16[1040,128]{1,0:T(8,128)(2,1)S(1)}, u32[]{:S(2)}, u32[]{:S(2)}) collective-permute-start(bf16[1040,128]{1,0:T(8,128)(2,1)S(1)} %shard_map.115), channel_id=1, source_target_pairs={{0,96},{1,33},{2,98},{3,35},{4,100},{5,37},{6,102},{7,39},{8,104},... | collective-permute-start | bytes 798728 | tf_op jit(solution)/shard_map/ppermute | solution.py:47
  54.1 0.0 collective-permute-start.1
  54.1 1.3 collective-permute-start.2
  55.4 0.7 shard_map.114.p0
  56.1 9.8 %collective-permute-done.3.p3 = bf16[1040,128]{1,0:T(8,128)(2,1)S(1)} collective-permute-done((bf16[1040,128]{1,0:T(8,128)(2,1)S(1)}, bf16[1040,128]{1,0:T(8,128)(2,1)S(1)}, u32[]{:S(2)}, u32[]{:S(2)}) %collective-permute-start.3) | collective-permute-done | bytes 266272 | tf_op jit(solution)/shard_map/ppermute | solution.py:47
  65.9 0.0 collective-permute-done.1.p1
  65.9 1.5 %collective-permute-done.2.p2 = bf16[1040,128]{1,0:T(8,128)(2,1)S(1)} collective-permute-done((bf16[1040,128]{1,0:T(8,128)(2,1)S(1)}, bf16[1040,128]{1,0:T(8,128)(2,1)S(1)}, u32[]{:S(2)}, u32[]{:S(2)}) %collective-permute-start.2) | collective-permute-done | bytes 266272 | tf_op jit(solution)/shard_map/ppermute | solution.py:47
  67.5 0.0 copy-done.5
  67.5 0.3 shard_map.116.b0
  67.7 0.9 collective-permute-start.8
  68.6 8.1 %collective-permute-done.8.b1 = bf16[1040,128]{1,0:T(8,128)(2,1)S(1)} collective-permute-done((bf16[1040,128]{1,0:T(8,128)(2,1)S(1)}, bf16[1040,128]{1,0:T(8,128)(2,1)S(1)}, u32[]{:S(2)}, u32[]{:S(2)}) %collective-permute-start.8) | collective-permute-done | bytes 266272 | tf_op jit(solution)/shard_map/ppermute | solution.py:47
  76.7 2.4 %shard_map.119 = (f32[16,400,128]{2,1,0:T(8,128)S(1)}, bf16[16,400,128]{2,1,0:T(8,128)(2,1)S(1)}) custom-call(s32[4]{0:T(128)S(1)} %pad_add_fusion.place_ref, bf16[1040,128]{1,0:T(8,128)(2,1)S(1)} %shard_map.116.b0, bf16[1040,128]{1,0:T(8,128)(2,1)S(1)} %collective-permute-done.8.b1, bf16[1024,512]{1,0:T(8,128)(2,1)S(1)} %get-tuple-element.21.pooled_ref, ...), custom_call_target="tpu_custom_call" | custom-call | flops 2147483648 | bytes 6291456 | tf_op jit(solution)/shard_map/pallas_call | solution.py:59
  79.1 0.1 collective-permute-start.9
  79.2 3.5 %collective-permute-start.4 = (bf16[1040,128]{1,0:T(8,128)(2,1)S(1)}, bf16[1040,128]{1,0:T(8,128)(2,1)S(1)}, u32[]{:S(2)}, u32[]{:S(2)}) collective-permute-start(bf16[1040,128]{1,0:T(8,128)(2,1)S(1)} %shard_map.116.b0), channel_id=1, source_target_pairs={{0,96},{1,33},{2,98},{3,35},{4,100},{5,37},{6,102},{7,39},{8,104},... | collective-permute-start | bytes 798728 | tf_op jit(solution)/shard_map/ppermute | solution.py:47
  82.7 0.0 collective-permute-start.5
  82.7 0.6 shard_map.118
  83.4 0.2 collective-permute-start.7
  83.6 5.4 %collective-permute-done.4.b2 = bf16[1040,128]{1,0:T(8,128)(2,1)S(1)} collective-permute-done((bf16[1040,128]{1,0:T(8,128)(2,1)S(1)}, bf16[1040,128]{1,0:T(8,128)(2,1)S(1)}, u32[]{:S(2)}, u32[]{:S(2)}) %collective-permute-start.4) | collective-permute-done | bytes 266272 | tf_op jit(solution)/shard_map/ppermute | solution.py:47
  88.9 1.4 %collective-permute-done.5.b3 = bf16[1040,128]{1,0:T(8,128)(2,1)S(1)} collective-permute-done((bf16[1040,128]{1,0:T(8,128)(2,1)S(1)}, bf16[1040,128]{1,0:T(8,128)(2,1)S(1)}, u32[]{:S(2)}, u32[]{:S(2)}) %collective-permute-start.5) | collective-permute-done | bytes 266272 | tf_op jit(solution)/shard_map/ppermute | solution.py:47
  90.3 0.9 shard_map.117
  91.2 0.1 collective-permute-start.6
  91.3 0.5 collective-permute-start.10
  91.8 0.1 collective-permute-start.11
  91.9 0.0 collective-permute-done.7.partner_ref
  91.9 1.7 %collective-permute-done.10.p2 = bf16[1040,128]{1,0:T(8,128)(2,1)S(1)} collective-permute-done((bf16[1040,128]{1,0:T(8,128)(2,1)S(1)}, bf16[1040,128]{1,0:T(8,128)(2,1)S(1)}, u32[]{:S(2)}, u32[]{:S(2)}) %collective-permute-start.10) | collective-permute-done | bytes 266272 | tf_op jit(solution)/shard_map/ppermute | solution.py:47
  93.6 0.4 collective-permute-done.11.p3
  94.0 0.0 collective-permute-done.9.other_ref
  94.0 0.8 shard_map.120.weights_ref
  94.8 0.0 collective-permute-done.6.their_products
  94.8 1.7 %shard_map.121 = bf16[16,400,128]{2,1,0:T(8,128)(2,1)} custom-call(bf16[256,1024]{1,0:T(8,128)(2,1)S(1)} %get-tuple-element.24.own_products, bf16[256,1024]{1,0:T(8,128)(2,1)S(1)} %collective-permute-done.6.their_products, bf16[1536,256]{1,0:T(8,128)(2,1)S(1)} %get-tuple-element.25.own_ref, bf16[1536,256]{1,0:T(8,128)(2,1)S(1)} %collective-permute-done.7.partner_ref, ...), custom_call_target="tpu_custom_call" | custom-call | flops 536870912 | bytes 4194304 | tf_op jit(solution)/shard_map/pallas_call | solution.py:59
  96.5 3.7 %all-to-all-start.1 = ((bf16[16,400,128]{2,1,0:T(8,128)(2,1)}), bf16[16,400,128]{2,1,0:T(8,128)(2,1)S(1)}, u32[]{:S(2)}, u32[]{:S(2)}) async-start(bf16[16,400,128]{2,1,0:T(8,128)(2,1)} %shard_map.121), calls=%async_computation.1 | async-start | bytes 3276800 | tf_op jit(solution)/shard_map/all_to_all | solution.py:485
  100.2 0.0 copy-start.1
  100.3 2.2 %copy-done.1 = bf16[512,4096]{1,0:T(8,128)(2,1)S(1)} copy-done((bf16[512,4096]{1,0:T(8,128)(2,1)S(1)}, bf16[512,4096]{1,0:T(8,128)(2,1)}, u32[]{:S(2)}) %copy-start.1) | copy-done | bytes 4194328
  102.4 0.7 shard_map.122
  103.1 23.9 %all-to-all-done.1.in_ref = bf16[16,400,128]{2,1,0:T(8,128)(2,1)S(1)} async-done(((bf16[16,400,128]{2,1,0:T(8,128)(2,1)}), bf16[16,400,128]{2,1,0:T(8,128)(2,1)S(1)}, u32[]{:S(2)}, u32[]{:S(2)}) %all-to-all-start.1) | async-done | bytes 1638432 | tf_op jit(solution)/shard_map/all_to_all | solution.py:485
  127.1 0.9 shard_map.123
  (1 shorter events, 0.0 us)
Async XLA Ops:
  0.7 45.0 %copy-start.2 = (bf16[4096,512]{1,0:T(8,128)(2,1)S(1)}, bf16[4096,512]{1,0:T(8,128)(2,1)}, u32[]{:S(2)}) copy-start(bf16[4096,512]{1,0:T(8,128)(2,1)} %down_ref.1) | copy-start | bytes 12582916
  3.9 41.8 %copy-start = (bf16[512,4096]{1,0:T(8,128)(2,1)S(1)}, bf16[512,4096]{1,0:T(8,128)(2,1)}, u32[]{:S(2)}) copy-start(bf16[512,4096]{1,0:T(8,128)(2,1)} %up_ref.3) | copy-start | bytes 12582916
  3.9 41.8 %copy-start.3 = (f32[4096]{0:T(1024)S(1)}, f32[4096]{0:T(1024)}, u32[]{:S(2)}) copy-start(f32[4096]{0:T(1024)} %param.12) | copy-start | bytes 49156
  3.9 41.8 %copy-start.4 = (f32[4096]{0:T(1024)S(1)}, f32[4096]{0:T(1024)}, u32[]{:S(2)}) copy-start(f32[4096]{0:T(1024)} %param.11) | copy-start | bytes 49156
  45.5 2.0 %collective-permute-start = (bf16[2048,128]{1,0:T(8,128)(2,1)S(1)}, bf16[2048,128]{1,0:T(8,128)(2,1)S(1)}, u32[]{:S(2)}, u32[]{:S(2)}) collective-permute-start(bf16[2048,128]{1,0:T(8,128)(2,1)S(1)} %slice.4), channel_id=1, source_target_pairs={{0,1},{1,0},{2,3},{3,2},{4,5},{5,4},{6,7},{7,6},{8,9},{9,8},{10,11... | collective-permute-start | bytes 1572872 | tf_op jit(solution)/shard_map/ppermute | solution.py:47
  50.0 17.4 %copy-start.5 = (s32[128]{0:T(128)S(1)}, s32[128]{0:T(128)}, u32[]{:S(2)}) copy-start(s32[128]{0:T(128)} %param.13) | copy-start | bytes 1540
  50.0 15.9 %collective-permute-start.3 = (bf16[1040,128]{1,0:T(8,128)(2,1)S(1)}, bf16[1040,128]{1,0:T(8,128)(2,1)S(1)}, u32[]{:S(2)}, u32[]{:S(2)}) collective-permute-start(bf16[1040,128]{1,0:T(8,128)(2,1)S(1)} %shard_map.115), channel_id=1, source_target_pairs={{0,96},{1,33},{2,98},{3,35},{4,100},{5,37},{6,102},{7,39},{8,104},... | collective-permute-start | bytes 798728 | tf_op jit(solution)/shard_map/ppermute | solution.py:47
  54.1 11.8 %collective-permute-start.1 = (bf16[1040,128]{1,0:T(8,128)(2,1)S(1)}, bf16[1040,128]{1,0:T(8,128)(2,1)S(1)}, u32[]{:S(2)}, u32[]{:S(2)}) collective-permute-start(bf16[1040,128]{1,0:T(8,128)(2,1)S(1)} %get-tuple-element.22), channel_id=1, source_target_pairs={{0,64},{1,65},{2,66},{3,67},{4,68},{5,69},{6,70},{7,71},{8,72},{9,... | collective-permute-start | bytes 798728 | tf_op jit(solution)/shard_map/ppermute | solution.py:47
  54.1 13.3 %collective-permute-start.2 = (bf16[1040,128]{1,0:T(8,128)(2,1)S(1)}, bf16[1040,128]{1,0:T(8,128)(2,1)S(1)}, u32[]{:S(2)}, u32[]{:S(2)}) collective-permute-start(bf16[1040,128]{1,0:T(8,128)(2,1)S(1)} %get-tuple-element.23), channel_id=1, source_target_pairs={{0,32},{1,97},{2,34},{3,99},{4,36},{5,101},{6,38},{7,103},{8,40},{... | collective-permute-start | bytes 798728 | tf_op jit(solution)/shard_map/ppermute | solution.py:47
  67.7 9.0 %collective-permute-start.8 = (bf16[1040,128]{1,0:T(8,128)(2,1)S(1)}, bf16[1040,128]{1,0:T(8,128)(2,1)S(1)}, u32[]{:S(2)}, u32[]{:S(2)}) collective-permute-start(bf16[1040,128]{1,0:T(8,128)(2,1)S(1)} %shard_map.116.b0), channel_id=1, source_target_pairs={{0,64},{1,65},{2,66},{3,67},{4,68},{5,69},{6,70},{7,71},{8,72},{9,... | collective-permute-start | bytes 798728 | tf_op jit(solution)/shard_map/ppermute | solution.py:47
  79.1 14.8 %collective-permute-start.9 = (bf16[16,400,128]{2,1,0:T(8,128)(2,1)S(1)}, bf16[16,400,128]{2,1,0:T(8,128)(2,1)S(1)}, u32[]{:S(2)}, u32[]{:S(2)}) collective-permute-start(bf16[16,400,128]{2,1,0:T(8,128)(2,1)S(1)} %get-tuple-element.28), channel_id=1, source_target_pairs={{0,1},{1,0},{2,3},{3,2},{4,5},{5,4},{6,7},{7,6},{8,9},{9,8},{10,11... | collective-permute-start | bytes 4915208 | tf_op jit(solution)/shard_map/ppermute | solution.py:47
  79.2 9.7 %collective-permute-start.4 = (bf16[1040,128]{1,0:T(8,128)(2,1)S(1)}, bf16[1040,128]{1,0:T(8,128)(2,1)S(1)}, u32[]{:S(2)}, u32[]{:S(2)}) collective-permute-start(bf16[1040,128]{1,0:T(8,128)(2,1)S(1)} %shard_map.116.b0), channel_id=1, source_target_pairs={{0,96},{1,33},{2,98},{3,35},{4,100},{5,37},{6,102},{7,39},{8,104},... | collective-permute-start | bytes 798728 | tf_op jit(solution)/shard_map/ppermute | solution.py:47
  82.7 7.6 %collective-permute-start.5 = (bf16[1040,128]{1,0:T(8,128)(2,1)S(1)}, bf16[1040,128]{1,0:T(8,128)(2,1)S(1)}, u32[]{:S(2)}, u32[]{:S(2)}) collective-permute-start(bf16[1040,128]{1,0:T(8,128)(2,1)S(1)} %shard_map.116.b0), channel_id=1, source_target_pairs={{0,32},{1,97},{2,34},{3,99},{4,36},{5,101},{6,38},{7,103},{8,40},{... | collective-permute-start | bytes 798728 | tf_op jit(solution)/shard_map/ppermute | solution.py:47
  83.4 8.5 %collective-permute-start.7 = (bf16[1536,256]{1,0:T(8,128)(2,1)S(1)}, bf16[1536,256]{1,0:T(8,128)(2,1)S(1)}, u32[]{:S(2)}, u32[]{:S(2)}) collective-permute-start(bf16[1536,256]{1,0:T(8,128)(2,1)S(1)} %get-tuple-element.26), channel_id=1, source_target_pairs={{0,1},{1,0},{2,3},{3,2},{4,5},{5,4},{6,7},{7,6},{8,9},{9,8},{10,11... | collective-permute-start | bytes 2359304 | tf_op jit(solution)/shard_map/ppermute | solution.py:47
  91.2 3.6 %collective-permute-start.6 = (bf16[256,1024]{1,0:T(8,128)(2,1)S(1)}, bf16[256,1024]{1,0:T(8,128)(2,1)S(1)}, u32[]{:S(2)}, u32[]{:S(2)}) collective-permute-start(bf16[256,1024]{1,0:T(8,128)(2,1)S(1)} %get-tuple-element.24.own_products), channel_id=1, source_target_pairs={{0,1},{1,0},{2,3},{3,2},{4,5},{5,4},{6,7},{7,6},{8,9},{9,8},{10,11... | collective-permute-start | bytes 1572872 | tf_op jit(solution)/shard_map/ppermute | solution.py:47
  91.3 2.3 %collective-permute-start.10 = (bf16[1040,128]{1,0:T(8,128)(2,1)S(1)}, bf16[1040,128]{1,0:T(8,128)(2,1)S(1)}, u32[]{:S(2)}, u32[]{:S(2)}) collective-permute-start(bf16[1040,128]{1,0:T(8,128)(2,1)S(1)} %collective-permute-done.4.b2), channel_id=1, source_target_pairs={{0,1},{1,0},{2,3},{3,2},{4,5},{5,4},{6,7},{7,6},{8,9},{9,8},{10,11... | collective-permute-start | bytes 798728 | tf_op jit(solution)/shard_map/ppermute | solution.py:47
  91.8 2.2 %collective-permute-start.11 = (bf16[1040,128]{1,0:T(8,128)(2,1)S(1)}, bf16[1040,128]{1,0:T(8,128)(2,1)S(1)}, u32[]{:S(2)}, u32[]{:S(2)}) collective-permute-start(bf16[1040,128]{1,0:T(8,128)(2,1)S(1)} %collective-permute-done.5.b3), channel_id=1, source_target_pairs={{0,1},{1,0},{2,3},{3,2},{4,5},{5,4},{6,7},{7,6},{8,9},{9,8},{10,11... | collective-permute-start | bytes 798728 | tf_op jit(solution)/shard_map/ppermute | solution.py:47
  96.5 30.5 %all-to-all-start.1 = ((bf16[16,400,128]{2,1,0:T(8,128)(2,1)}), bf16[16,400,128]{2,1,0:T(8,128)(2,1)S(1)}, u32[]{:S(2)}, u32[]{:S(2)}) async-start(bf16[16,400,128]{2,1,0:T(8,128)(2,1)} %shard_map.121), calls=%async_computation.1 | async-start | bytes 3276800 | tf_op jit(solution)/shard_map/all_to_all | solution.py:485
  100.2 2.2 %copy-start.1 = (bf16[512,4096]{1,0:T(8,128)(2,1)S(1)}, bf16[512,4096]{1,0:T(8,128)(2,1)}, u32[]{:S(2)}) copy-start(bf16[512,4096]{1,0:T(8,128)(2,1)} %up_ref.3) | copy-start | bytes 12582916

commit v4 on v2

--- a/solution.py
+++ b/solution.py
@@ -82,10 +82,10 @@
             return pltpu.make_async_copy(counts_ref.at[:, pl.ds(start, strip)], held.at[y, n], sems.at[y, n])
 
         slab_copy = pltpu.make_async_copy(slab_ref, slab_s, slab_sem)
-        slab_copy.start()
         for y in range(NY):
             for n in range(NZ):
                 copy(y, n).start(priority=n % 2)
+        slab_copy.start()
         slab_copy.wait()
         for k in range(PEERS):
             half = k % NC
@@ -416,10 +416,10 @@
 def finish(shares, own, up_own):
     def body(in_ref, own_ref, up_ref, slab_out, down_out, up_out, bias_out, out_out):
         def total(at):
-            held = in_ref[0, at, :].astype(F32)
-            for i in range(1, NY * NX):
-                held = held + in_ref[i, at, :].astype(F32)
-            return held
+            held = [(in_ref[i, at, :] + in_ref[i + 1, at, :]).astype(F32) for i in range(0, NY * NX, 2)]
+            while len(held) > 1:
+                held = [a + b for a, b in zip(held[::2], held[1::2])]
+            return held[0]
 
         slab_out[:, :128] = total(slice(0, ROWS))
         slab_out[:, 128:] = total(slice(ROWS, 2 * ROWS))

time: 128 us -> 128 us (level)
  no operation moved by 1% of the time
where the time goes in v4:
time: 128 us
  waiting for transfers between devices  50.6 us (40%)
  blocking collectives  41.6 us (32%)
  Pallas kernels  16.5 us (13%)
  starting transfers between devices  16.3 us (13%)
  local copies, waits for them, and re-layouts  2.25 us (2%)
    all_to_all x1, blocking collectives, local(): lax.all_to_all(sent, PLANE, 0, 0, tiled=True)  41.6 us
    ppermute x12, waiting for transfers between devices, shift(): return lax.ppermute(value, ALL, pairs)  26.7 us
    all_to_all x1, waiting for transfers between devices, local(): shares = lax.all_to_all(summed, ('y', 'x'), 0, 0, tiled=True)  23.9 us
    pallas_call x14, Pallas kernels, call(): pl.pallas_call(body, in_specs=specs or [pl.BlockSpec(memory_space=pltpu.V...  16.5 us
    ppermute x12, starting transfers between devices, shift(): return lax.ppermute(value, ALL, pairs)  12.6 us
    all_to_all x1, starting transfers between devices, local(): shares = lax.all_to_all(summed, ('y', 'x'), 0, 0, tiled=True)  3.71 us
  transfers between devices with their start and end apart: 13, of which 9 were waited for; matrix products, arithmetic and copies ran while one was open for 0% of the time, Pallas kernels for 4%

profile of v4, /device:TPU:0, one launch (start us, length us, event | category | flops | bytes accessed | tf_op | source)
XLA Modules:
  0.0 128.0 jit_solution(11135930897391899425)
XLA Ops:
  0.6 0.1 pad_add_fusion.place_ref
  0.7 0.0 copy-start.2
  0.7 3.1 %shard_map.110 = bf16[32,64,640]{2,1,0:T(8,128)(2,1)S(1)} custom-call(s32[4]{0:T(128)S(1)} %pad_add_fusion.place_ref, s32[64,16384]{1,0:T(8,128)} %bitcast.22, bf16[64,256]{1,0:T(8,128)(2,1)} %slab_ref.1), custom_call_target="tpu_custom_call" | custom-call | tf_op jit(solution)/shard_map/pallas_call | solution.py:59
  3.9 0.0 copy-start
  3.9 0.0 copy-start.3
  3.9 0.0 copy-start.4
  3.9 41.6 %all_to_all.10 = bf16[32,64,640]{2,1,0:T(8,128)(2,1)S(1)} all-to-all(bf16[32,64,640]{2,1,0:T(8,128)(2,1)S(1)} %shard_map.110), channel_id=1, replica_groups=mesh['z'=4,'y'=4,'x'=4,'c'=2] {'y','x','c'}, dimensions={0} | all-to-all | bytes 5242880 | tf_op jit(solution)/shard_map/all_to_all | solution.py:460
  45.5 0.2 collective-permute-start
  45.7 0.0 copy-done.2
  45.7 0.0 copy-done
  45.7 0.0 copy-done.3
  45.7 0.0 copy-done.4
  45.7 1.2 shard_map.112.rows_ref
  46.9 0.5 shard_map.111.half_ref
  47.3 0.1 collective-permute-done.other_ref
  47.5 1.8 %shard_map.113 = (bf16[1024,512]{1,0:T(8,128)(2,1)S(1)}, bf16[1040,128]{1,0:T(8,128)(2,1)S(1)}) custom-call(s32[4]{0:T(128)S(1)} %pad_add_fusion.place_ref, bf16[2048,640]{1,0:T(8,128)(2,1)S(1)} %bitcast.14, bf16[2048,128]{1,0:T(8,128)(2,1)S(1)} %collective-permute-done.other_ref, bf16[512,512]{1,0:T(8,128)(2,1)S(1)} %shard_map.111.half_ref, ...), custom_call_target="tpu_custom_call" | custom-call | flops 3221225472 | bytes 4194304 | tf_op jit(solution)/shard_map/pallas_call | solution.py:59
  49.3 0.8 shard_map.115
  50.1 0.0 copy-start.5
  50.1 4.0 %collective-permute-start.1 = (bf16[1040,128]{1,0:T(8,128)(2,1)S(1)}, bf16[1040,128]{1,0:T(8,128)(2,1)S(1)}, u32[]{:S(2)}, u32[]{:S(2)}) collective-permute-start(bf16[1040,128]{1,0:T(8,128)(2,1)S(1)} %get-tuple-element.23), channel_id=1, source_target_pairs={{0,64},{1,65},{2,66},{3,67},{4,68},{5,69},{6,70},{7,71},{8,72},{9,... | collective-permute-start | bytes 798728 | tf_op jit(solution)/shard_map/ppermute | solution.py:47
  54.0 0.7 collective-permute-start.3
  54.8 1.3 %collective-permute-start.2 = (bf16[1040,128]{1,0:T(8,128)(2,1)S(1)}, bf16[1040,128]{1,0:T(8,128)(2,1)S(1)}, u32[]{:S(2)}, u32[]{:S(2)}) collective-permute-start(bf16[1040,128]{1,0:T(8,128)(2,1)S(1)} %get-tuple-element.24), channel_id=1, source_target_pairs={{0,32},{1,97},{2,34},{3,99},{4,36},{5,101},{6,38},{7,103},{8,40},{... | collective-permute-start | bytes 798728 | tf_op jit(solution)/shard_map/ppermute | solution.py:47
  56.1 0.7 shard_map.114.p0
  56.8 4.5 %collective-permute-done.1.p1 = bf16[1040,128]{1,0:T(8,128)(2,1)S(1)} collective-permute-done((bf16[1040,128]{1,0:T(8,128)(2,1)S(1)}, bf16[1040,128]{1,0:T(8,128)(2,1)S(1)}, u32[]{:S(2)}, u32[]{:S(2)}) %collective-permute-start.1) | collective-permute-done | bytes 266272 | tf_op jit(solution)/shard_map/ppermute | solution.py:47
  61.3 6.0 %collective-permute-done.3.p3 = bf16[1040,128]{1,0:T(8,128)(2,1)S(1)} collective-permute-done((bf16[1040,128]{1,0:T(8,128)(2,1)S(1)}, bf16[1040,128]{1,0:T(8,128)(2,1)S(1)}, u32[]{:S(2)}, u32[]{:S(2)}) %collective-permute-start.3) | collective-permute-done | bytes 266272 | tf_op jit(solution)/shard_map/ppermute | solution.py:47
  67.4 0.0 collective-permute-done.2.p2
  67.4 0.0 copy-done.5
  67.4 0.3 shard_map.116.b0
  67.6 2.1 %collective-permute-start.8 = (bf16[1040,128]{1,0:T(8,128)(2,1)S(1)}, bf16[1040,128]{1,0:T(8,128)(2,1)S(1)}, u32[]{:S(2)}, u32[]{:S(2)}) collective-permute-start(bf16[1040,128]{1,0:T(8,128)(2,1)S(1)} %shard_map.116.b0), channel_id=1, source_target_pairs={{0,64},{1,65},{2,66},{3,67},{4,68},{5,69},{6,70},{7,71},{8,72},{9,... | collective-permute-start | bytes 798728 | tf_op jit(solution)/shard_map/ppermute | solution.py:47
  69.7 7.2 %collective-permute-done.8.b1 = bf16[1040,128]{1,0:T(8,128)(2,1)S(1)} collective-permute-done((bf16[1040,128]{1,0:T(8,128)(2,1)S(1)}, bf16[1040,128]{1,0:T(8,128)(2,1)S(1)}, u32[]{:S(2)}, u32[]{:S(2)}) %collective-permute-start.8) | collective-permute-done | bytes 266272 | tf_op jit(solution)/shard_map/ppermute | solution.py:47
  76.9 2.4 %shard_map.119 = (f32[16,400,128]{2,1,0:T(8,128)S(1)}, bf16[16,400,128]{2,1,0:T(8,128)(2,1)S(1)}) custom-call(s32[4]{0:T(128)S(1)} %pad_add_fusion.place_ref, bf16[1040,128]{1,0:T(8,128)(2,1)S(1)} %shard_map.116.b0, bf16[1040,128]{1,0:T(8,128)(2,1)S(1)} %collective-permute-done.8.b1, bf16[1024,512]{1,0:T(8,128)(2,1)S(1)} %get-tuple-element.22.pooled_ref, ...), custom_call_target="tpu_custom_call" | custom-call | flops 2147483648 | bytes 6291456 | tf_op jit(solution)/shard_map/pallas_call | solution.py:59
  79.3 0.1 collective-permute-start.9
  79.4 3.3 %collective-permute-start.4 = (bf16[1040,128]{1,0:T(8,128)(2,1)S(1)}, bf16[1040,128]{1,0:T(8,128)(2,1)S(1)}, u32[]{:S(2)}, u32[]{:S(2)}) collective-permute-start(bf16[1040,128]{1,0:T(8,128)(2,1)S(1)} %shard_map.116.b0), channel_id=1, source_target_pairs={{0,96},{1,33},{2,98},{3,35},{4,100},{5,37},{6,102},{7,39},{8,104},... | collective-permute-start | bytes 798728 | tf_op jit(solution)/shard_map/ppermute | solution.py:47
  82.7 0.0 collective-permute-start.5
  82.7 0.6 shard_map.118
  83.4 0.2 collective-permute-start.7
  83.6 5.4 %collective-permute-done.4.b2 = bf16[1040,128]{1,0:T(8,128)(2,1)S(1)} collective-permute-done((bf16[1040,128]{1,0:T(8,128)(2,1)S(1)}, bf16[1040,128]{1,0:T(8,128)(2,1)S(1)}, u32[]{:S(2)}, u32[]{:S(2)}) %collective-permute-start.4) | collective-permute-done | bytes 266272 | tf_op jit(solution)/shard_map/ppermute | solution.py:47
  89.0 1.4 %collective-permute-done.5.b3 = bf16[1040,128]{1,0:T(8,128)(2,1)S(1)} collective-permute-done((bf16[1040,128]{1,0:T(8,128)(2,1)S(1)}, bf16[1040,128]{1,0:T(8,128)(2,1)S(1)}, u32[]{:S(2)}, u32[]{:S(2)}) %collective-permute-start.5) | collective-permute-done | bytes 266272 | tf_op jit(solution)/shard_map/ppermute | solution.py:47
  90.3 0.9 shard_map.117
  91.2 0.1 collective-permute-start.6
  91.3 0.5 collective-permute-start.10
  91.8 0.1 collective-permute-start.11
  91.9 0.0 collective-permute-done.7.partner_ref
  91.9 1.7 %collective-permute-done.10.p2 = bf16[1040,128]{1,0:T(8,128)(2,1)S(1)} collective-permute-done((bf16[1040,128]{1,0:T(8,128)(2,1)S(1)}, bf16[1040,128]{1,0:T(8,128)(2,1)S(1)}, u32[]{:S(2)}, u32[]{:S(2)}) %collective-permute-start.10) | collective-permute-done | bytes 266272 | tf_op jit(solution)/shard_map/ppermute | solution.py:47
  93.6 0.4 collective-permute-done.11.p3
  94.0 0.0 collective-permute-done.9.other_ref
  94.0 0.8 shard_map.120.weights_ref
  94.8 0.0 collective-permute-done.6.their_products
  94.8 1.7 %shard_map.121 = bf16[16,400,128]{2,1,0:T(8,128)(2,1)} custom-call(bf16[256,1024]{1,0:T(8,128)(2,1)S(1)} %get-tuple-element.26.own_products, bf16[256,1024]{1,0:T(8,128)(2,1)S(1)} %collective-permute-done.6.their_products, bf16[1536,256]{1,0:T(8,128)(2,1)S(1)} %get-tuple-element.27.own_ref, bf16[1536,256]{1,0:T(8,128)(2,1)S(1)} %collective-permute-done.7.partner_ref, ...), custom_call_target="tpu_custom_call" | custom-call | flops 536870912 | bytes 4194304 | tf_op jit(solution)/shard_map/pallas_call | solution.py:59
  96.6 3.7 %all-to-all-start.1 = ((bf16[16,400,128]{2,1,0:T(8,128)(2,1)}), bf16[16,400,128]{2,1,0:T(8,128)(2,1)S(1)}, u32[]{:S(2)}, u32[]{:S(2)}) async-start(bf16[16,400,128]{2,1,0:T(8,128)(2,1)} %shard_map.121), calls=%async_computation.1 | async-start | bytes 3276800 | tf_op jit(solution)/shard_map/all_to_all | solution.py:486
  100.3 0.0 copy-start.1
  100.3 2.2 %copy-done.1 = bf16[512,4096]{1,0:T(8,128)(2,1)S(1)} copy-done((bf16[512,4096]{1,0:T(8,128)(2,1)S(1)}, bf16[512,4096]{1,0:T(8,128)(2,1)}, u32[]{:S(2)}) %copy-start.1) | copy-done | bytes 4194328
  102.5 0.7 shard_map.122
  103.2 23.9 %all-to-all-done.1.in_ref = bf16[16,400,128]{2,1,0:T(8,128)(2,1)S(1)} async-done(((bf16[16,400,128]{2,1,0:T(8,128)(2,1)}), bf16[16,400,128]{2,1,0:T(8,128)(2,1)S(1)}, u32[]{:S(2)}, u32[]{:S(2)}) %all-to-all-start.1) | async-done | bytes 1638432 | tf_op jit(solution)/shard_map/all_to_all | solution.py:486
  127.1 0.9 shard_map.123
  (1 shorter events, 0.0 us)
Async XLA Ops:
  0.7 45.0 %copy-start.2 = (bf16[4096,512]{1,0:T(8,128)(2,1)S(1)}, bf16[4096,512]{1,0:T(8,128)(2,1)}, u32[]{:S(2)}) copy-start(bf16[4096,512]{1,0:T(8,128)(2,1)} %down_ref.1) | copy-start | bytes 12582916
  3.9 41.8 %copy-start = (bf16[512,4096]{1,0:T(8,128)(2,1)S(1)}, bf16[512,4096]{1,0:T(8,128)(2,1)}, u32[]{:S(2)}) copy-start(bf16[512,4096]{1,0:T(8,128)(2,1)} %up_ref.3) | copy-start | bytes 12582916
  3.9 41.8 %copy-start.3 = (f32[4096]{0:T(1024)S(1)}, f32[4096]{0:T(1024)}, u32[]{:S(2)}) copy-start(f32[4096]{0:T(1024)} %param.12) | copy-start | bytes 49156
  3.9 41.8 %copy-start.4 = (f32[4096]{0:T(1024)S(1)}, f32[4096]{0:T(1024)}, u32[]{:S(2)}) copy-start(f32[4096]{0:T(1024)} %param.11) | copy-start | bytes 49156
  45.5 2.0 %collective-permute-start = (bf16[2048,128]{1,0:T(8,128)(2,1)S(1)}, bf16[2048,128]{1,0:T(8,128)(2,1)S(1)}, u32[]{:S(2)}, u32[]{:S(2)}) collective-permute-start(bf16[2048,128]{1,0:T(8,128)(2,1)S(1)} %slice.4), channel_id=1, source_target_pairs={{0,1},{1,0},{2,3},{3,2},{4,5},{5,4},{6,7},{7,6},{8,9},{9,8},{10,11... | collective-permute-start | bytes 1572872 | tf_op jit(solution)/shard_map/ppermute | solution.py:47
  50.1 17.3 %copy-start.5 = (s32[128]{0:T(128)S(1)}, s32[128]{0:T(128)}, u32[]{:S(2)}) copy-start(s32[128]{0:T(128)} %param.13) | copy-start | bytes 1540
  50.1 11.2 %collective-permute-start.1 = (bf16[1040,128]{1,0:T(8,128)(2,1)S(1)}, bf16[1040,128]{1,0:T(8,128)(2,1)S(1)}, u32[]{:S(2)}, u32[]{:S(2)}) collective-permute-start(bf16[1040,128]{1,0:T(8,128)(2,1)S(1)} %get-tuple-element.23), channel_id=1, source_target_pairs={{0,64},{1,65},{2,66},{3,67},{4,68},{5,69},{6,70},{7,71},{8,72},{9,... | collective-permute-start | bytes 798728 | tf_op jit(solution)/shard_map/ppermute | solution.py:47
  54.0 13.3 %collective-permute-start.3 = (bf16[1040,128]{1,0:T(8,128)(2,1)S(1)}, bf16[1040,128]{1,0:T(8,128)(2,1)S(1)}, u32[]{:S(2)}, u32[]{:S(2)}) collective-permute-start(bf16[1040,128]{1,0:T(8,128)(2,1)S(1)} %get-tuple-element.25), channel_id=1, source_target_pairs={{0,96},{1,33},{2,98},{3,35},{4,100},{5,37},{6,102},{7,39},{8,104},... | collective-permute-start | bytes 798728 | tf_op jit(solution)/shard_map/ppermute | solution.py:47
  54.8 12.6 %collective-permute-start.2 = (bf16[1040,128]{1,0:T(8,128)(2,1)S(1)}, bf16[1040,128]{1,0:T(8,128)(2,1)S(1)}, u32[]{:S(2)}, u32[]{:S(2)}) collective-permute-start(bf16[1040,128]{1,0:T(8,128)(2,1)S(1)} %get-tuple-element.24), channel_id=1, source_target_pairs={{0,32},{1,97},{2,34},{3,99},{4,36},{5,101},{6,38},{7,103},{8,40},{... | collective-permute-start | bytes 798728 | tf_op jit(solution)/shard_map/ppermute | solution.py:47
  67.6 9.3 %collective-permute-start.8 = (bf16[1040,128]{1,0:T(8,128)(2,1)S(1)}, bf16[1040,128]{1,0:T(8,128)(2,1)S(1)}, u32[]{:S(2)}, u32[]{:S(2)}) collective-permute-start(bf16[1040,128]{1,0:T(8,128)(2,1)S(1)} %shard_map.116.b0), channel_id=1, source_target_pairs={{0,64},{1,65},{2,66},{3,67},{4,68},{5,69},{6,70},{7,71},{8,72},{9,... | collective-permute-start | bytes 798728 | tf_op jit(solution)/shard_map/ppermute | solution.py:47
  79.3 14.7 %collective-permute-start.9 = (bf16[16,400,128]{2,1,0:T(8,128)(2,1)S(1)}, bf16[16,400,128]{2,1,0:T(8,128)(2,1)S(1)}, u32[]{:S(2)}, u32[]{:S(2)}) collective-permute-start(bf16[16,400,128]{2,1,0:T(8,128)(2,1)S(1)} %get-tuple-element.30), channel_id=1, source_target_pairs={{0,1},{1,0},{2,3},{3,2},{4,5},{5,4},{6,7},{7,6},{8,9},{9,8},{10,11... | collective-permute-start | bytes 4915208 | tf_op jit(solution)/shard_map/ppermute | solution.py:47
  79.4 9.5 %collective-permute-start.4 = (bf16[1040,128]{1,0:T(8,128)(2,1)S(1)}, bf16[1040,128]{1,0:T(8,128)(2,1)S(1)}, u32[]{:S(2)}, u32[]{:S(2)}) collective-permute-start(bf16[1040,128]{1,0:T(8,128)(2,1)S(1)} %shard_map.116.b0), channel_id=1, source_target_pairs={{0,96},{1,33},{2,98},{3,35},{4,100},{5,37},{6,102},{7,39},{8,104},... | collective-permute-start | bytes 798728 | tf_op jit(solution)/shard_map/ppermute | solution.py:47
  82.7 7.6 %collective-permute-start.5 = (bf16[1040,128]{1,0:T(8,128)(2,1)S(1)}, bf16[1040,128]{1,0:T(8,128)(2,1)S(1)}, u32[]{:S(2)}, u32[]{:S(2)}) collective-permute-start(bf16[1040,128]{1,0:T(8,128)(2,1)S(1)} %shard_map.116.b0), channel_id=1, source_target_pairs={{0,32},{1,97},{2,34},{3,99},{4,36},{5,101},{6,38},{7,103},{8,40},{... | collective-permute-start | bytes 798728 | tf_op jit(solution)/shard_map/ppermute | solution.py:47
  83.4 8.5 %collective-permute-start.7 = (bf16[1536,256]{1,0:T(8,128)(2,1)S(1)}, bf16[1536,256]{1,0:T(8,128)(2,1)S(1)}, u32[]{:S(2)}, u32[]{:S(2)}) collective-permute-start(bf16[1536,256]{1,0:T(8,128)(2,1)S(1)} %get-tuple-element.28), channel_id=1, source_target_pairs={{0,1},{1,0},{2,3},{3,2},{4,5},{5,4},{6,7},{7,6},{8,9},{9,8},{10,11... | collective-permute-start | bytes 2359304 | tf_op jit(solution)/shard_map/ppermute | solution.py:47
  91.2 3.6 %collective-permute-start.6 = (bf16[256,1024]{1,0:T(8,128)(2,1)S(1)}, bf16[256,1024]{1,0:T(8,128)(2,1)S(1)}, u32[]{:S(2)}, u32[]{:S(2)}) collective-permute-start(bf16[256,1024]{1,0:T(8,128)(2,1)S(1)} %get-tuple-element.26.own_products), channel_id=1, source_target_pairs={{0,1},{1,0},{2,3},{3,2},{4,5},{5,4},{6,7},{7,6},{8,9},{9,8},{10,11... | collective-permute-start | bytes 1572872 | tf_op jit(solution)/shard_map/ppermute | solution.py:47
  91.3 2.3 %collective-permute-start.10 = (bf16[1040,128]{1,0:T(8,128)(2,1)S(1)}, bf16[1040,128]{1,0:T(8,128)(2,1)S(1)}, u32[]{:S(2)}, u32[]{:S(2)}) collective-permute-start(bf16[1040,128]{1,0:T(8,128)(2,1)S(1)} %collective-permute-done.4.b2), channel_id=1, source_target_pairs={{0,1},{1,0},{2,3},{3,2},{4,5},{5,4},{6,7},{7,6},{8,9},{9,8},{10,11... | collective-permute-start | bytes 798728 | tf_op jit(solution)/shard_map/ppermute | solution.py:47
  91.8 2.2 %collective-permute-start.11 = (bf16[1040,128]{1,0:T(8,128)(2,1)S(1)}, bf16[1040,128]{1,0:T(8,128)(2,1)S(1)}, u32[]{:S(2)}, u32[]{:S(2)}) collective-permute-start(bf16[1040,128]{1,0:T(8,128)(2,1)S(1)} %collective-permute-done.5.b3), channel_id=1, source_target_pairs={{0,1},{1,0},{2,3},{3,2},{4,5},{5,4},{6,7},{7,6},{8,9},{9,8},{10,11... | collective-permute-start | bytes 798728 | tf_op jit(solution)/shard_map/ppermute | solution.py:47
  96.6 30.5 %all-to-all-start.1 = ((bf16[16,400,128]{2,1,0:T(8,128)(2,1)}), bf16[16,400,128]{2,1,0:T(8,128)(2,1)S(1)}, u32[]{:S(2)}, u32[]{:S(2)}) async-start(bf16[16,400,128]{2,1,0:T(8,128)(2,1)} %shard_map.121), calls=%async_computation.1 | async-start | bytes 3276800 | tf_op jit(solution)/shard_map/all_to_all | solution.py:486
  100.3 2.2 %copy-start.1 = (bf16[512,4096]{1,0:T(8,128)(2,1)S(1)}, bf16[512,4096]{1,0:T(8,128)(2,1)}, u32[]{:S(2)}) copy-start(bf16[512,4096]{1,0:T(8,128)(2,1)} %up_ref.3) | copy-start | bytes 12582916
